TPU v7x, 256 devices: a whole 4x4x8 slice. The times are simulated.
256 devices in a mesh: rve: 8 (over x, y_hi), slab: 32 (over y_lo, z, core).
Axes of the slice: x: 4, y: 4 (y_hi: 2, y_lo: 2; y = y_hi * 2 + y_lo), z: 8, core: 2. Of those that a mesh axis runs over, the one named last changes fastest.
Arguments:
- displacement: float32 [128, 3, 256, 256], P('slab', None, 'rve'), parts along dimension 2, may hold values from -6 to 6
- load: float32 [128, 3, 256, 256], P('slab', None, 'rve'), parts along dimension 2, may hold values from -24 to 24
- phase: int32 [128, 256, 256], P('slab', 'rve'), parts along dimension 1, may hold values from 0 to 2
- moduli: float32 [2, 3], replicated, may hold values from 0.5 to 4
Outputs:
- solution: float32 [128, 3, 256, 256], P('slab', None, 'rve'), parts along dimension 2
- residual: float32 [128, 3, 256, 256], P('slab', None, 'rve'), parts along dimension 2
There are 8 independent parts, one for each index of `rve`. A program takes and returns all parts, laid end to end along the dimension named above; an argument that names none is the same for every part. Nothing has to cross between parts.
All inputs are finite; a program needn't handle non-finite values.
Results may differ from a plain program's by a relative error of at most 0.00002.
Values sent between devices are 32-bit elements; how exact they have to be, the bound alone decides.
No kernel may reach another device: no remote copies, remote signals or barrier semaphores. Data moves between devices by JAX's collectives and lax.ppermute only.
A program may use at most 64 MiB of HBM per device.

v0:
```python
import jax
import jax.numpy as jnp
from jax import lax
from jax.sharding import PartitionSpec as P

SWEEPS = 6


def padded_2(array, sides, width):
    for axis, dim in sides:
        peers, length = (lax.axis_size(axis), array.shape[dim])
        up = [(i, (i + 1) % peers) for i in range(peers)]
        down = [(j, i) for i, j in up]
        last = lax.slice_in_dim(array, length - width, length, axis=dim)
        first = lax.slice_in_dim(array, 0, width, axis=dim)
        before = lax.ppermute(last, axis, up)
        after = lax.ppermute(first, axis, down)
        array = jnp.concatenate([before, array, after], axis=dim)
    return array


def plus_next(value, axis):
    return value + jnp.roll(value, -1, axis)


def minus_next(value, axis):
    return jnp.roll(value, -1, axis) - value


def plus_prev(value, axis):
    return value + jnp.roll(value, 1, axis)


def prev_minus(value, axis):
    return jnp.roll(value, 1, axis) - value


def materials(phase, moduli):
    lame = jnp.zeros(phase.shape, jnp.float32)
    shear = jnp.zeros(phase.shape, jnp.float32)
    for index in range(moduli.shape[1]):
        select = (phase == index).astype(jnp.float32)
        lame = lame + select * moduli[0, index]
        shear = shear + select * moduli[1, index]
    return (lame, shear)


def element_terms(lower, upper, lame, shear):
    total = lower + upper
    jump = upper - lower
    grad_x = 0.25 * minus_next(plus_next(total, -1), -2)
    grad_y = 0.25 * plus_next(minus_next(total, -1), -2)
    grad_z = 0.25 * plus_next(plus_next(jump, -1), -2)
    trace = grad_x[:, 0] + grad_y[:, 1] + grad_z[:, 2]
    normal_x = lame * trace + 2.0 * shear * grad_x[:, 0]
    normal_y = lame * trace + 2.0 * shear * grad_y[:, 1]
    normal_z = lame * trace + 2.0 * shear * grad_z[:, 2]
    shear_xy = shear * (grad_y[:, 0] + grad_x[:, 1])
    shear_xz = shear * (grad_z[:, 0] + grad_x[:, 2])
    shear_yz = shear * (grad_z[:, 1] + grad_y[:, 2])
    col_x = jnp.stack([normal_x, shear_xy, shear_xz], 1)
    col_y = jnp.stack([shear_xy, normal_y, shear_yz], 1)
    col_z = jnp.stack([shear_xz, shear_yz, normal_z], 1)
    inplane = 0.25 * (plus_prev(prev_minus(col_x, -2), -1) + plus_prev(prev_minus(col_y, -1), -2))
    vertical = 0.25 * plus_prev(plus_prev(col_z, -1), -2)
    return (inplane, vertical)


def apply_padded(field, lame_part, shear_part):
    inplane, vertical = element_terms(field[:-1], field[1:], lame_part, shear_part)
    return inplane[1:] + inplane[:-1] + vertical[:-1] - vertical[1:]


def field_padded(field):
    return padded_2(field, (("slab", 0),), 2)


def diagonal_of(lame_ext, shear_ext):
    stiff = lame_ext + 4.0 * shear_ext
    planar = plus_prev(plus_prev(stiff, -1), -2)
    return ((planar[1:] + planar[:-1]) / 16.0)[:, None]


def on_device(displacement, load, phase, moduli):
    lame, shear = materials(phase, moduli)
    stacked = jnp.concatenate([load, lame[:, None], shear[:, None]], 1)
    padded = padded_2(stacked, (("slab", 0),), 2)
    load_ext = padded[1:-1, 0:3]
    lame_ext = padded[:-1, 3]
    shear_ext = padded[:-1, 4]
    diagonal = diagonal_of(lame_ext, shear_ext)
    field = displacement
    for pair in range(SWEEPS // 2):
        wide = field_padded(field)
        wide = wide[1:-1] + 0.5 * (load_ext - apply_padded(wide, lame_ext, shear_ext)) / diagonal
        field = (
            wide[1:-1]
            + 0.5
            * (load_ext[1:-1] - apply_padded(wide, lame_ext[1:-1], shear_ext[1:-1]))
            / diagonal[1:-1]
        )
    wide = field_padded(field)[1:-1]
    remain = load_ext[1:-1] - apply_padded(wide, lame_ext[1:-1], shear_ext[1:-1])
    return (field, remain)


def solution(mesh):
    in_specs = (
        P("slab", None, "rve", None),
        P("slab", None, "rve", None),
        P("slab", "rve", None),
        P(),
    )
    out_specs = (P("slab", None, "rve", None), P("slab", None, "rve", None))
    return jax.shard_map(
        on_device, mesh=mesh, in_specs=in_specs, out_specs=out_specs, check_vma=False
    )
```

profile of v0, /device:TPU:2, one launch (start us, length us, event | category | flops | bytes accessed | tf_op | source)
XLA Modules:
  0.0 71.3 jit_solution(2988910101918538095)
XLA Ops:
  0.6 1.1 %fusion.109 = (f32[2,3,32,256]{3,2,1,0:T(8,128)S(1)}, f32[2,3,32,256]{3,2,1,0:T(8,128)S(1)}) fusion(f32[4,3,32,256]{3,2,1,0:T(8,128)} %param.4), kind=kLoop, calls=%fused_computation.314 | loop fusion | bytes 786432 | tf_op jit(solution)/shard_map/slice | solution.py:15
  1.8 1.6 %fusion.110 = (f32[1,1]{1,0:T(1,128)}, f32[1,1]{1,0:T(1,128)}, f32[1,1]{1,0:T(1,128)}, f32[1,1]{1,0:T(1,128)}, f32[1,1]{1,0:T(1,128)}, /*index=5*/f32[1,1]{1,0:T(1,128)}) fusion(f32[2,3]{1,0:T(2,128)} %param.7), kind=kLoop, calls=%fused_computation.315 | loop fusion | bytes 48 | tf_op jit(solution)/shard_map/slice | solution.py:44
  3.4 2.9 %add_bitcast_fusion.2 = (f32[4,1,32,256]{3,2,1,0:T(8,128)S(1)}, pred[4,32,256]{2,1,0:T(8,128)(4,1)S(1)}, pred[4,32,256]{2,1,0:T(8,128)(4,1)S(1)}, pred[4,32,256]{2,1,0:T(8,128)(4,1)S(1)}) fusion(f32[]{:T(128)} %bitcast.2, f32[]{:T(128)} %bitcast.1, f32[]{:T(128)} %bitcast, s32[4,32,256]{2,1,0:T(8,128)} %param.6), kind=kLoop, calls=%fused_computation.302 | loop fusion | flops 262144 | bytes 360460 | tf_op jit(solution)/shard_map/broadcast_in_dim | solution.py:86
  6.3 2.0 %add_bitcast_fusion.1 = f32[4,1,32,256]{3,2,1,0:T(8,128)S(1)} fusion(pred[4,32,256]{2,1,0:T(8,128)(4,1)S(1)} %get-tuple-element.24, pred[4,32,256]{2,1,0:T(8,128)(4,1)S(1)} %get-tuple-element.23, pred[4,32,256]{2,1,0:T(8,128)(4,1)S(1)} %get-tuple-element.22, f32[]{:T(128)} %bitcast.7, f32[]{:T(128)} %bitcast.6, f32[]{:T(128)} %bitcast.5), kind=kLoop, calls=%fused_computation.301 | loop fusion | flops 163840 | bytes 229388 | tf_op jit(solution)/shard_map/broadcast_in_dim | solution.py:86
  8.4 2.1 %collective-permute-start.2 = (f32[2,5,32,256]{3,2,1,0:T(8,128)S(1)}, f32[2,5,32,256]{3,2,1,0:T(8,128)S(1)}, u32[]{:S(2)}, u32[]{:S(2)}) collective-permute-start(f32[2,5,32,256]{3,2,1,0:T(8,128)S(1)} %get-tuple-element.70), channel_id=1, source_target_pairs={{0,1},{1,2},{2,3},{3,4},{4,5},{5,6},{6,7},{7,8},{8,9},{9,10},{10,1... | collective-permute-start | bytes 983048 | tf_op jit(solution)/shard_map/ppermute | solution.py:16
  10.5 4.4 %collective-permute-start.3 = (f32[2,5,32,256]{3,2,1,0:T(8,128)S(1)}, f32[2,5,32,256]{3,2,1,0:T(8,128)S(1)}, u32[]{:S(2)}, u32[]{:S(2)}) collective-permute-start(f32[2,5,32,256]{3,2,1,0:T(8,128)S(1)} %get-tuple-element.71), channel_id=1, source_target_pairs={{1,0},{2,1},{3,2},{4,3},{5,4},{6,5},{7,6},{8,7},{9,8},{10,9},{11,1... | collective-permute-start | bytes 983048 | tf_op jit(solution)/shard_map/ppermute | solution.py:17
  14.9 0.7 collective-permute-start.1
  15.6 6.0 %collective-permute-done.1 = f32[2,3,32,256]{3,2,1,0:T(8,128)S(1)} collective-permute-done((f32[2,3,32,256]{3,2,1,0:T(8,128)S(1)}, f32[2,3,32,256]{3,2,1,0:T(8,128)S(1)}, u32[]{:S(2)}, u32[]{:S(2)}) %collective-permute-start.1) | collective-permute-done | bytes 196640 | tf_op jit(solution)/shard_map/ppermute | solution.py:17
  21.7 0.2 slice.1259
  22.0 0.2 slice.1267
  22.3 0.2 maximum_add_fusion.1
  22.6 0.2 fusion.59
  23.2 0.3 fusion
  23.9 0.3 multiply_add_fusion.7
  24.3 0.3 pad_maximum_fusion.5
  24.9 0.5 maximum_subtract_fusion.2
  25.8 0.4 fusion.4
  26.3 0.3 fusion.29
  26.7 0.2 slice.1303
  27.2 0.2 slice.1311
  28.2 0.2 pad_maximum_fusion.20
  28.7 0.4 maximum_subtract_fusion.11
  29.3 0.3 fusion.34
  29.9 4.3 %collective-permute-start.5 = (f32[2,3,32,256]{3,2,1,0:T(8,128)S(1)}, f32[2,3,32,256]{3,2,1,0:T(8,128)S(1)}, u32[]{:S(2)}, u32[]{:S(2)}) collective-permute-start(f32[2,3,32,256]{3,2,1,0:T(8,128)S(1)} %get-tuple-element.89), channel_id=1, source_target_pairs={{1,0},{2,1},{3,2},{4,3},{5,4},{6,5},{7,6},{8,7},{9,8},{10,9},{11,1... | collective-permute-start | bytes 589832 | tf_op jit(solution)/shard_map/ppermute | solution.py:17
  34.1 3.1 %collective-permute-done.4 = f32[2,3,32,256]{3,2,1,0:T(8,128)S(1)} collective-permute-done((f32[2,3,32,256]{3,2,1,0:T(8,128)S(1)}, f32[2,3,32,256]{3,2,1,0:T(8,128)S(1)}, u32[]{:S(2)}, u32[]{:S(2)}) %collective-permute-start.4) | collective-permute-done | bytes 196640 | tf_op jit(solution)/shard_map/ppermute | solution.py:16
  37.6 0.2 slice.1344
  37.9 0.2 fusion.57
  38.2 0.2 slice.1352
  38.4 0.2 maximum_add_fusion.8
  39.2 0.3 multiply_add_fusion.4
  39.6 0.3 pad_maximum_fusion.9
  40.2 0.5 maximum_subtract_fusion.5
  41.1 0.4 fusion.10
  41.5 0.3 fusion.25
  41.9 0.2 slice.1382
  42.3 0.2 slice.1390
  43.1 0.2 multiply_add_fusion.16
  43.3 0.2 pad_maximum_fusion.24
  43.8 0.4 maximum_subtract_fusion.14
  44.4 0.3 fusion.40
  45.0 4.3 %collective-permute-start.7 = (f32[2,3,32,256]{3,2,1,0:T(8,128)S(1)}, f32[2,3,32,256]{3,2,1,0:T(8,128)S(1)}, u32[]{:S(2)}, u32[]{:S(2)}) collective-permute-start(f32[2,3,32,256]{3,2,1,0:T(8,128)S(1)} %get-tuple-element.87), channel_id=1, source_target_pairs={{1,0},{2,1},{3,2},{4,3},{5,4},{6,5},{7,6},{8,7},{9,8},{10,9},{11,1... | collective-permute-start | bytes 589832 | tf_op jit(solution)/shard_map/ppermute | solution.py:17
  49.3 3.0 %collective-permute-done.6 = f32[2,3,32,256]{3,2,1,0:T(8,128)S(1)} collective-permute-done((f32[2,3,32,256]{3,2,1,0:T(8,128)S(1)}, f32[2,3,32,256]{3,2,1,0:T(8,128)S(1)}, u32[]{:S(2)}, u32[]{:S(2)}) %collective-permute-start.6) | collective-permute-done | bytes 196640 | tf_op jit(solution)/shard_map/ppermute | solution.py:16
  52.8 0.2 slice.1422
  53.0 0.2 fusion.55
  53.3 0.2 slice.1430
  53.6 0.2 maximum_add_fusion.15
  54.4 0.3 multiply_add_fusion.1
  54.8 0.3 pad_maximum_fusion.13
  55.4 0.5 maximum_subtract_fusion.8
  56.3 0.4 fusion.16
  56.7 0.3 fusion.21
  57.0 0.2 slice.1460
  57.5 0.2 slice.1468
  58.5 0.2 pad_maximum_fusion.28
  59.0 0.4 maximum_subtract_fusion.17
  59.6 0.3 fusion.46
  60.2 4.1 %collective-permute-start.9 = (f32[2,3,32,256]{3,2,1,0:T(8,128)S(1)}, f32[2,3,32,256]{3,2,1,0:T(8,128)S(1)}, u32[]{:S(2)}, u32[]{:S(2)}) collective-permute-start(f32[2,3,32,256]{3,2,1,0:T(8,128)S(1)} %get-tuple-element.84), channel_id=1, source_target_pairs={{1,0},{2,1},{3,2},{4,3},{5,4},{6,5},{7,6},{8,7},{9,8},{10,9},{11,1... | collective-permute-start | bytes 589832 | tf_op jit(solution)/shard_map/ppermute | solution.py:17
  64.3 3.3 %collective-permute-done.8 = f32[2,3,32,256]{3,2,1,0:T(8,128)S(1)} collective-permute-done((f32[2,3,32,256]{3,2,1,0:T(8,128)S(1)}, f32[2,3,32,256]{3,2,1,0:T(8,128)S(1)}, u32[]{:S(2)}, u32[]{:S(2)}) %collective-permute-start.8) | collective-permute-done | bytes 196640 | tf_op jit(solution)/shard_map/ppermute | solution.py:16
  67.7 0.2 slice.1497
  68.1 0.2 slice.1505
  69.1 0.2 pad_maximum_fusion.32
  69.6 0.4 maximum_subtract_fusion.20
  70.2 0.3 fusion.52
  70.5 0.8 %fusion.60 = f32[4,3,32,256]{3,2,1,0:T(8,128)} fusion(f32[4,3,32,256]{3,2,1,0:T(8,128)S(1)} %copy-done, f32[5,3,32,256]{3,2,1,0:T(8,128)S(1)} %fusion.53, f32[5,3,32,256]{3,2,1,0:T(8,128)S(1)} %fusion.52), kind=kLoop, calls=%fused_computation.186 | loop fusion | flops 393216 | bytes 2359296 | tf_op jit(solution)/shard_map/sub | solution.py:103
  (186 shorter events, 12.5 us)
Async XLA Ops:
  0.6 7.6 %copy-start = (f32[4,3,32,256]{3,2,1,0:T(8,128)S(1)}, f32[4,3,32,256]{3,2,1,0:T(8,128)}, u32[]{:S(2)}) copy-start(f32[4,3,32,256]{3,2,1,0:T(8,128)} %param.5) | copy-start | bytes 1179652
  1.7 13.8 %collective-permute-start = (f32[2,3,32,256]{3,2,1,0:T(8,128)S(1)}, f32[2,3,32,256]{3,2,1,0:T(8,128)S(1)}, u32[]{:S(2)}, u32[]{:S(2)}) collective-permute-start(f32[2,3,32,256]{3,2,1,0:T(8,128)S(1)} %get-tuple-element.91), channel_id=1, source_target_pairs={{0,1},{1,2},{2,3},{3,4},{4,5},{5,6},{6,7},{7,8},{8,9},{9,10},{10,1... | collective-permute-start | bytes 589832 | tf_op jit(solution)/shard_map/ppermute | solution.py:16
  8.3 7.3 %copy-start.2 = (f32[4,3,32,256]{3,2,1,0:T(8,128)S(1)}, f32[4,3,32,256]{3,2,1,0:T(8,128)}, u32[]{:S(2)}) copy-start(f32[4,3,32,256]{3,2,1,0:T(8,128)} %param.4) | copy-start | bytes 1179652
  8.4 15.1 %collective-permute-start.2 = (f32[2,5,32,256]{3,2,1,0:T(8,128)S(1)}, f32[2,5,32,256]{3,2,1,0:T(8,128)S(1)}, u32[]{:S(2)}, u32[]{:S(2)}) collective-permute-start(f32[2,5,32,256]{3,2,1,0:T(8,128)S(1)} %get-tuple-element.70), channel_id=1, source_target_pairs={{0,1},{1,2},{2,3},{3,4},{4,5},{5,6},{6,7},{7,8},{8,9},{9,10},{10,1... | collective-permute-start | bytes 983048 | tf_op jit(solution)/shard_map/ppermute | solution.py:16
  10.5 13.0 %collective-permute-start.3 = (f32[2,5,32,256]{3,2,1,0:T(8,128)S(1)}, f32[2,5,32,256]{3,2,1,0:T(8,128)S(1)}, u32[]{:S(2)}, u32[]{:S(2)}) collective-permute-start(f32[2,5,32,256]{3,2,1,0:T(8,128)S(1)} %get-tuple-element.71), channel_id=1, source_target_pairs={{1,0},{2,1},{3,2},{4,3},{5,4},{6,5},{7,6},{8,7},{9,8},{10,9},{11,1... | collective-permute-start | bytes 983048 | tf_op jit(solution)/shard_map/ppermute | solution.py:17
  14.9 6.7 %collective-permute-start.1 = (f32[2,3,32,256]{3,2,1,0:T(8,128)S(1)}, f32[2,3,32,256]{3,2,1,0:T(8,128)S(1)}, u32[]{:S(2)}, u32[]{:S(2)}) collective-permute-start(f32[2,3,32,256]{3,2,1,0:T(8,128)S(1)} %get-tuple-element.90), channel_id=1, source_target_pairs={{1,0},{2,1},{3,2},{4,3},{5,4},{6,5},{7,6},{8,7},{9,8},{10,9},{11,1... | collective-permute-start | bytes 589832 | tf_op jit(solution)/shard_map/ppermute | solution.py:17
  29.8 7.4 %collective-permute-start.4 = (f32[2,3,32,256]{3,2,1,0:T(8,128)S(1)}, f32[2,3,32,256]{3,2,1,0:T(8,128)S(1)}, u32[]{:S(2)}, u32[]{:S(2)}) collective-permute-start(f32[2,3,32,256]{3,2,1,0:T(8,128)S(1)} %get-tuple-element.88), channel_id=1, source_target_pairs={{0,1},{1,2},{2,3},{3,4},{4,5},{5,6},{6,7},{7,8},{8,9},{9,10},{10,1... | collective-permute-start | bytes 589832 | tf_op jit(solution)/shard_map/ppermute | solution.py:16
  29.9 7.5 %collective-permute-start.5 = (f32[2,3,32,256]{3,2,1,0:T(8,128)S(1)}, f32[2,3,32,256]{3,2,1,0:T(8,128)S(1)}, u32[]{:S(2)}, u32[]{:S(2)}) collective-permute-start(f32[2,3,32,256]{3,2,1,0:T(8,128)S(1)} %get-tuple-element.89), channel_id=1, source_target_pairs={{1,0},{2,1},{3,2},{4,3},{5,4},{6,5},{7,6},{8,7},{9,8},{10,9},{11,1... | collective-permute-start | bytes 589832 | tf_op jit(solution)/shard_map/ppermute | solution.py:17
  44.9 7.4 %collective-permute-start.6 = (f32[2,3,32,256]{3,2,1,0:T(8,128)S(1)}, f32[2,3,32,256]{3,2,1,0:T(8,128)S(1)}, u32[]{:S(2)}, u32[]{:S(2)}) collective-permute-start(f32[2,3,32,256]{3,2,1,0:T(8,128)S(1)} %get-tuple-element.86), channel_id=1, source_target_pairs={{0,1},{1,2},{2,3},{3,4},{4,5},{5,6},{6,7},{7,8},{8,9},{9,10},{10,1... | collective-permute-start | bytes 589832 | tf_op jit(solution)/shard_map/ppermute | solution.py:16
  45.0 7.5 %collective-permute-start.7 = (f32[2,3,32,256]{3,2,1,0:T(8,128)S(1)}, f32[2,3,32,256]{3,2,1,0:T(8,128)S(1)}, u32[]{:S(2)}, u32[]{:S(2)}) collective-permute-start(f32[2,3,32,256]{3,2,1,0:T(8,128)S(1)} %get-tuple-element.87), channel_id=1, source_target_pairs={{1,0},{2,1},{3,2},{4,3},{5,4},{6,5},{7,6},{8,7},{9,8},{10,9},{11,1... | collective-permute-start | bytes 589832 | tf_op jit(solution)/shard_map/ppermute | solution.py:17
  60.1 7.8 %copy-start.1 = (f32[4,3,32,256]{3,2,1,0:T(8,128)}, f32[4,3,32,256]{3,2,1,0:T(8,128)S(1)}, u32[]{:S(2)}) copy-start(f32[4,3,32,256]{3,2,1,0:T(8,128)S(1)} %fusion.64) | copy-start | bytes 1179652
  60.1 7.4 %collective-permute-start.8 = (f32[2,3,32,256]{3,2,1,0:T(8,128)S(1)}, f32[2,3,32,256]{3,2,1,0:T(8,128)S(1)}, u32[]{:S(2)}, u32[]{:S(2)}) collective-permute-start(f32[2,3,32,256]{3,2,1,0:T(8,128)S(1)} %get-tuple-element.85), channel_id=1, source_target_pairs={{0,1},{1,2},{2,3},{3,4},{4,5},{5,6},{6,7},{7,8},{8,9},{9,10},{10,1... | collective-permute-start | bytes 589832 | tf_op jit(solution)/shard_map/ppermute | solution.py:16
  60.2 7.4 %collective-permute-start.9 = (f32[2,3,32,256]{3,2,1,0:T(8,128)S(1)}, f32[2,3,32,256]{3,2,1,0:T(8,128)S(1)}, u32[]{:S(2)}, u32[]{:S(2)}) collective-permute-start(f32[2,3,32,256]{3,2,1,0:T(8,128)S(1)} %get-tuple-element.84), channel_id=1, source_target_pairs={{1,0},{2,1},{3,2},{4,3},{5,4},{6,5},{7,6},{8,7},{9,8},{10,9},{11,1... | collective-permute-start | bytes 589832 | tf_op jit(solution)/shard_map/ppermute | solution.py:17
where the time goes:
time: 71.6 us; the launch traced here: 71.3 us
  other arithmetic  22.4 us (31%)
  starting transfers between devices  20.2 us (28%)
  waiting for transfers between devices  15.6 us (22%)
  local copies, waits for them, and re-layouts  11 us (15%)
  between operations  2.22 us (3%)
    ppermute x5, starting transfers between devices, padded_2(): after = lax.ppermute(first, axis, down)  17.7 us
    ppermute x5, waiting for transfers between devices, padded_2(): before = lax.ppermute(last, axis, up)  9.4 us
    ppermute x5, waiting for transfers between devices, padded_2(): after = lax.ppermute(first, axis, down)  6.21 us
    broadcast_in_dim x2, other arithmetic, on_device(): stacked = jnp.concatenate([load, lame[:, None], shear[:, None]], 1)  4.83 us
    slice x56, local copies, waits for them, and re-layouts, plus_next(): return value + jnp.roll(value, -1, axis)  4.21 us
    sub x7, other arithmetic, prev_minus(): return jnp.roll(value, 1, axis) - value  2.96 us
    ppermute x5, starting transfers between devices, padded_2(): before = lax.ppermute(last, axis, up)  2.43 us
    add x14, other arithmetic, plus_next(): return value + jnp.roll(value, -1, axis)  2.38 us
  transfers between devices with their start and end apart: 10, of which 6 were waited for; matrix products, arithmetic and copies ran while one was open for 12% of the time, Pallas kernels for 0%

commit v1 on v0

v1 whole, which is shorter than its diff:
```python
import jax
import jax.numpy as jnp
from jax import lax
from jax.experimental import pallas as pl
from jax.experimental.pallas import tpu as pltpu
from jax.sharding import PartitionSpec as P


OWN = 4
DEPTH = 6
INNER = 3
NODES = DEPTH + OWN + INNER
LAYERS = 16
N0 = DEPTH
L0 = 8

VMEM = pl.BlockSpec(memory_space=pltpu.VMEM)
SMEM = pl.BlockSpec(memory_space=pltpu.SMEM)
HBM = pl.BlockSpec(memory_space=pltpu.HBM)
ROW = (4, 8, 256)


def f32(*shape):
    return jax.ShapeDtypeStruct(shape + ROW, jnp.float32)


def even_rows():
    return lax.broadcasted_iota(jnp.int32, (8, 128), 0) % 2 == 0


def load_raw(ref, index, r):
    a = ref[index + (pl.ds(r, 8, stride=8), slice(None))]
    b = ref[index + (pl.ds(r + 4, 8, stride=8), slice(None))]
    even = even_rows()
    low = jnp.where(even, a, pltpu.roll(b, 1, 0))
    high = jnp.where(even, pltpu.roll(a, 7, 0), b)
    return jnp.concatenate([low, high], axis=1)


def store_raw(ref, index, r, value):
    low, high = value[:, :128], value[:, 128:]
    even = even_rows()
    ref[index + (pl.ds(r, 8, stride=8), slice(None))] = jnp.where(even, low, pltpu.roll(high, 1, 0))
    ref[index + (pl.ds(r + 4, 8, stride=8), slice(None))] = jnp.where(even, pltpu.roll(low, 7, 0), high)


def y_next(v):
    return pltpu.roll(v, 255, 1)


def y_prev(v):
    return pltpu.roll(v, 1, 1)


def x_prev(rows, r):
    return rows[r - 1] if r > 0 else pltpu.roll(rows[3], 1, 0)


def y_stage(sm, get, m):
    for c in range(3):
        for r in range(4):
            d = get(m, c, r)
            n = y_next(d)
            sm[m + L0, c, r] = d + n
            sm[m + L0, 3 + c, r] = n - d


def stress_step(sm, st, lm, m, get):
    first = prev = None

    def stress(z, nxt, r):
        x0, y1, z2, _, _, e, pd, qd = z
        gxx = nxt[0] - x0
        gyy = nxt[1] + y1
        gzz = nxt[2] + z2
        lame, mu = lm[m + L0, 0, r], lm[m + L0, 1, r]
        lt = lame * (gxx + gyy + gzz)
        mu2 = mu + mu
        st[m + L0, 0, r] = lt + mu2 * gxx
        st[m + L0, 1, r] = mu * (nxt[3] + pd)
        st[m + L0, 2, r] = lt + mu2 * gyy
        st[m + L0, 3, r] = mu * (nxt[4] + qd)
        st[m + L0, 4, r] = mu * (nxt[5] + e)
        st[m + L0, 5, r] = lt + mu2 * gzz

    for r in range(4):
        s, my, j = [], [], []
        for c in range(3):
            d = get(m + 1, c, r)
            n = y_next(d)
            su, mu_ = d + n, n - d
            sl, ml = sm[m + L0, c, r], sm[m + L0, 3 + c, r]
            sm[m + 1 + L0, c, r] = su
            sm[m + 1 + L0, 3 + c, r] = mu_
            s.append(sl + su)
            my.append(ml + mu_)
            j.append(su - sl)
        z = (s[0], my[1], j[2], my[0] + s[1], j[0] + s[2], j[1] + my[2], my[0] - s[1], j[0] - s[2])
        if r == 0:
            first = z
        else:
            stress(prev, z, r - 1)
        prev = z
    stress(prev, tuple(pltpu.roll(v, 7, 0) for v in first[:6]), 3)


def node_sums(st, m, r, above, below):
    new = [st[m + L0, i, r] if above else None for i in range(6)]
    old = [st[m - 1 + L0, i, r] if below else None for i in range(6)]

    def plus(i):
        return new[i] if not below else old[i] if not above else new[i] + old[i]

    def minus(i):
        return -new[i] if not below else old[i] if not above else old[i] - new[i]

    xx, xy, yy, xz, yz = (plus(i) for i in range(5))
    dxz, dyz, dzz = (minus(i) for i in range(3, 6))
    return (
        (xx + dxz, xy + dyz, xz + dzz),
        (dxz - xx, dyz - xy, dzz - xz),
        (xy, yy, yz),
    )


def node_step(st, m, finish, above=True, below=True):
    first = prev = None

    def out(pq, pp, ph, r):
        for c in range(3):
            g = pp[c] + pq[1][c]
            hh = ph[c] + pq[2][c]
            finish(m, c, r, (g - hh) + y_prev(g + hh))

    for r in range(4):
        pq = node_sums(st, m, r, above, below)
        if r == 0:
            first = pq
        else:
            out(pq, prev[0], prev[2], r)
        prev = pq
    roll = lambda v: pltpu.roll(v, 1, 0)
    out(first, tuple(map(roll, prev[0])), tuple(map(roll, prev[2])), 0)


def advance(refs, s, lo, hi):
    R, W, LM, U, sm, st = refs
    src, dst = s % 2, (s + 1) % 2

    def get(m, c, r):
        return W[m + N0, r] * R[src, m + N0, c, r]

    def finisher(own):
        def finish(m, c, r, k):
            old = R[src, m + N0, c, r]
            R[dst, m + N0, c, r] = old - k
            if own:
                U[m, c, r] = U[m, c, r] + W[m + N0, r] * old

        return finish

    y_stage(sm, get, lo - 1)
    stress_step(sm, st, LM, lo - 1, get)
    stress_step(sm, st, LM, lo, get)

    for m in range(lo, hi):
        stress_step(sm, st, LM, m + 1, get)
        node_step(st, m, finisher(0 <= m < OWN))
    node_step(st, hi, finisher(0 <= hi < OWN))


def materials(LM, mod, load, m):
    for r in range(4):
        v = load(r)
        one, two = v == 1, v == 2
        for i in range(2):
            LM[m + L0, i, r] = jnp.where(two, mod[3 * i + 2], jnp.where(one, mod[3 * i + 1], mod[3 * i]))


def raw(ref, k):
    return lambda r: load_raw(ref, (k,), r)


def weights(W, LM, lo, hi):
    for m in range(lo, hi + 1):
        t = []
        for r in range(4):
            v = (LM[m - 1 + L0, 0, r] + LM[m + L0, 0, r]) + 4.0 * (LM[m - 1 + L0, 1, r] + LM[m + L0, 1, r])
            t.append(v)
        for r in range(4):
            v = t[r] + x_prev(t, r)
            W[m + N0, r] = 0.5 / (v + y_prev(v))


def sign_of(par):
    return (1 - 2 * par[0]).astype(jnp.float32)


def oriented(v, c, sign):
    return v * sign if c == 2 else v


def kernel_prep(par, mod_h, u_h, f_h, ph_h, PB, UV, FV, MOD, ph, mod, sem):
    odd = par[0]
    copies = [
        pltpu.make_async_copy(src, dst, sem.at[i])
        for i, (src, dst) in enumerate(((ph_h, ph), (u_h, UV), (mod_h, mod), (f_h, FV)))
    ]
    for copy in copies:
        copy.start()
    copies[0].wait()
    for k in range(4):
        PB[3 + k] = ph[k].astype(jnp.float32)
    copies[1].wait()
    for c in range(3):
        PB[c] = UV[3 * odd, c]
    copies[2].wait()
    for i in range(2):
        for j in range(3):
            MOD[3 * i + j] = jnp.full((8, 256), mod[i, j] * 0.0625, jnp.float32)
    copies[3].wait()


def kernel_own(par, mod, u, f, own, R, LM, U, PAY, sm, st):
    odd, sign = par[0], sign_of(par)
    plane = lambda m: jnp.where(odd == 1, 3 - m, m)
    for k in range(4):
        materials(LM, mod, raw(own, 3 + k), jnp.where(odd == 1, 2 - k, k))
    for m in range(4):
        for c in range(3):
            for r in range(4):
                U[m, c, r] = oriented(load_raw(u, (plane(m), c), r), c, sign)

    def get(m, c, r):
        return U[m, c, r]

    def finish(m, c, r, k):
        v = oriented(load_raw(f, (plane(m), c), r), c, sign) - k
        R[0, m + N0, c, r] = v
        PAY[m, c, r] = v

    y_stage(sm, get, 0)
    stress_step(sm, st, LM, 0, get)
    for m in range(3):
        if m < 2:
            stress_step(sm, st, LM, m + 1, get)
        node_step(st, m, finish, below=m > 0)


def kernel_rest(par, mod, f, own, ua, pa, r_in, lm_in, u_in, p_in, R, LM, U, PAY, uw, sm, st):
    odd, sign = par[0], sign_of(par)
    for k in range(4):
        materials(LM, mod, raw(pa, k), jnp.where(odd == 1, 6 - k, 4 + k))
    for c in range(3):
        for r in range(4):
            uw[0, c, r] = oriented(load_raw(ua, (3 * odd, c), r), c, sign)
    for j in range(3):
        for r in range(4):
            v = load_raw(pa, (jnp.where(odd == 1, 3 - j, max(j - 1, 0)),), r).astype(jnp.float32)
            if j == 0:
                v = jnp.where(odd == 1, v, load_raw(own, (6,), r))
            PAY[4, j, r] = v

    def get(m, c, r):
        return U[m, c, r] if m < 4 else uw[0, c, r]

    def finish(m, c, r, k):
        v = oriented(load_raw(f, (jnp.where(odd == 1, 0, 3), c), r), c, sign) - k
        R[0, m + N0, c, r] = v
        PAY[m, c, r] = v

    y_stage(sm, get, 2)
    stress_step(sm, st, LM, 2, get)
    stress_step(sm, st, LM, 3, get)
    node_step(st, 3, finish)


def kernel_setup(par, mod, pb, r_in, lm_in, u_in, R, LM, U, W, EDGE, uw, sm, st):
    odd, sign = par[0], sign_of(par)
    for c in range(3):
        for r in range(4):
            uw[0, c, r] = oriented(load_raw(pb, (c,), r), c, sign)
    for k in range(4):
        materials(LM, mod, raw(pb, 3 + k), jnp.where(odd == 1, -2 - k, k - 4))
    weights(W, LM, -3, 6)

    def get(m, c, r):
        return uw[0, c, r] if m == -1 else U[0, c, r]

    def keep(m, c, r, k):
        EDGE[c, r] = k

    def take(m, c, r, k):
        R[0, N0, c, r] = R[0, N0, c, r] - k

    y_stage(sm, get, -1)
    stress_step(sm, st, LM, -1, get)
    node_step(st, -1, keep, below=False)
    node_step(st, 0, take, above=False)


def kernel_near(a2, r_in, lm_in, u_in, w_in, R, LM, U, W, sm, st):
    for j in range(3):
        for c in range(3):
            v = a2[3 - j, c]
            R[0, 4 + j + N0, c] = -v if c == 2 else v
    refs = (R, W, LM, U, sm, st)
    advance(refs, 0, 1, 5)
    advance(refs, 1, 2, 4)
    advance(refs, 2, 3, 3)


def kernel_mid(mod, b2, edge, r_in, lm_in, u_in, w_in, R, LM, U, W, PAY, sm, st):
    for j in range(4):
        for c in range(3):
            v = b2[j, c]
            v = -v if c == 2 else v
            R[0, -1 - j + N0, c] = v - edge[c] if j == 0 else v
    for j in range(3):
        materials(LM, mod, lambda r: b2[4, j, r], -5 - j)
    weights(W, LM, -6, -4)
    refs = (R, W, LM, U, sm, st)
    advance(refs, 0, -3, 0)
    advance(refs, 1, -2, 1)
    advance(refs, 2, -1, 2)
    for j in range(3):
        for c in range(3):
            PAY[j, c] = R[1, 1 + j + N0, c]


def kernel_lead(r_in, lm_in, u_in, w_in, R, LM, U, W, sm, st):
    refs = (R, W, LM, U, sm, st)
    advance(refs, 3, 0, 2)
    advance(refs, 4, 1, 1)


def kernel_inner(a3, r_in, lm_in, u_in, w_in, R, LM, U, W, sm, st):
    for j in range(3):
        for c in range(3):
            v = a3[2 - j, c]
            R[1, 4 + j + N0, c] = -v if c == 2 else v
    refs = (R, W, LM, U, sm, st)
    advance(refs, 3, 3, 5)
    advance(refs, 4, 2, 4)
    advance(refs, 5, 2, 3)


def kernel_last(par, b3, r_in, lm_in, u_in, w_in, sol_h, res_h, R, LM, U, W, sm, st, sol, res, sem):
    odd, sign = par[0], sign_of(par)

    def put(m):
        k = jnp.where(odd == 1, 3 - m, m)
        for c in range(3):
            for r in range(4):
                store_raw(sol, (m, c), r, oriented(U[m, c, r], c, sign))
                store_raw(res, (m, c), r, oriented(R[0, m + N0, c, r], c, sign))
        copies = [
            pltpu.make_async_copy(src.at[m], dst.at[k], sem.at[2 * m + i])
            for i, (src, dst) in enumerate(((sol, sol_h), (res, res_h)))
        ]
        for copy in copies:
            copy.start()
        return copies

    started = put(2) + put(3)
    for j in range(2):
        for c in range(3):
            R[0, -5 - j + N0, c] = b3[1 - j, c]
    refs = (R, W, LM, U, sm, st)
    advance(refs, 0, -5, -4)
    advance(refs, 1, -4, -3)
    advance(refs, 2, -3, -2)
    advance(refs, 3, -2, -1)
    advance(refs, 4, -1, 0)
    advance(refs, 5, 0, 1)
    started = started + put(0) + put(1)
    for copy in started:
        copy.wait()


def call(kernel, in_specs, out_shape, scratch, alias, planes, extra=(), out_specs=None):
    return pl.pallas_call(
        kernel,
        out_shape=out_shape,
        in_specs=in_specs,
        out_specs=out_specs or tuple(VMEM for _ in out_shape),
        scratch_shapes=[pltpu.VMEM(s + ROW, jnp.float32) for s in scratch] + list(extra),
        input_output_aliases=alias,
        compiler_params=pltpu.CompilerParams(vmem_limit_bytes=14 << 20),
        cost_estimate=pl.CostEstimate(flops=planes * 700000, bytes_accessed=planes * 500000, transcendentals=0),
    )


def tiles(x):
    lead = x.shape[:-2]
    return x.reshape(lead + (4, 8, 2, 128)).swapaxes(-3, -2).reshape(lead + (64, 128))


def untiles(x):
    lead = x.shape[:-2]
    return x.reshape(lead + (4, 2, 8, 128)).swapaxes(-3, -2).reshape(lead + (32, 256))


def sweeps(displacement, load, phase, moduli):
    count = lax.axis_size("slab")
    odd = lax.bitwise_and(lax.axis_index("slab"), 1)
    par = odd.reshape(1).astype(jnp.int32)
    inside = [(i, i ^ 1) for i in range(count)]
    across = [(i, (i - 1) % count if i % 2 == 0 else (i + 1) % count) for i in range(count)]

    def send(v, pairs):
        return lax.ppermute(v, "slab", pairs)

    sm, st = (LAYERS, 6), (LAYERS, 6)
    R, LM, U, W = f32(2, NODES, 3), f32(LAYERS, 2), f32(OWN, 3), f32(NODES)
    state = (R, LM, U, W)
    dma = lambda n: pltpu.SemaphoreType.DMA((n,))
    block = lambda n, kind=jnp.float32: pltpu.VMEM((n, 64, 128), kind)
    shape = lambda n: jax.ShapeDtypeStruct((n, 64, 128), jnp.float32)
    in_hbm = lambda v: pltpu.with_memory_space_constraint(v, pltpu.HBM)
    u_t, f_t, ph_t = (in_hbm(tiles(v)) for v in (displacement, load, phase))
    moduli = in_hbm(moduli)

    ua = send(displacement, inside)
    pa = send(phase, inside)
    whole = jax.ShapeDtypeStruct((OWN, 3, 64, 128), jnp.float32)
    six = jax.ShapeDtypeStruct((6, 8, 256), jnp.float32)
    pb0, uv, fv, mod = call(
        kernel_prep,
        [SMEM] + [HBM] * 4,
        (shape(7), whole, whole, six),
        [],
        {},
        2,
        [block(4, jnp.int32), pltpu.SMEM((2, 3), jnp.float32), dma(4)],
    )(par, moduli, u_t, f_t, ph_t)
    pb = send(pb0, across)
    r, lm, u, pay = call(
        kernel_own, [SMEM] + [VMEM] * 4, (R, LM, U, f32(5, 3)), [sm, st], {}, 4
    )(par, mod, uv, fv, pb0)
    r, lm, u, pay = call(
        kernel_rest,
        [SMEM] + [VMEM] * 9,
        (R, LM, U, f32(5, 3)),
        [(1, 3), sm, st],
        {6: 0, 7: 1, 8: 2, 9: 3},
        2,
    )(par, mod, fv, pb0, tiles(ua), tiles(pa), r, lm, u, pay)
    b2 = send(pay, across)
    a2 = send(pay, inside)
    r, lm, u, w, edge = call(
        kernel_setup,
        [SMEM] + [VMEM] * 5,
        state + (f32(3),),
        [(1, 3), sm, st],
        {3: 0, 4: 1, 5: 2},
        4,
    )(par, mod, pb, r, lm, u)
    r, lm, u, w = call(
        kernel_near, [VMEM] * 5, state, [sm, st], {1: 0, 2: 1, 3: 2, 4: 3}, 11
    )(a2, r, lm, u, w)
    b3 = send(a2[2:4], across)
    r, lm, u, w, pay = call(
        kernel_mid, [VMEM] * 7, state + (f32(3, 3),), [sm, st], {3: 0, 4: 1, 5: 2, 6: 3}, 14
    )(mod, b2, edge, r, lm, u, w)
    a3 = send(pay, inside)
    r, lm, u, w = call(
        kernel_lead, [VMEM] * 4, state, [sm, st], {0: 0, 1: 1, 2: 2, 3: 3}, 6
    )(r, lm, u, w)
    r, lm, u, w = call(
        kernel_inner, [VMEM] * 5, state, [sm, st], {1: 0, 2: 1, 3: 2, 4: 3}, 10
    )(a3, r, lm, u, w)
    sol, res, _, _, _, _ = call(
        kernel_last,
        [SMEM] + [VMEM] * 5,
        (whole, whole) + state,
        [sm, st],
        {2: 2, 3: 3, 4: 4, 5: 5},
        18,
        [pltpu.VMEM((OWN, 3, 64, 128), jnp.float32)] * 2 + [dma(8)],
        (HBM, HBM) + (VMEM,) * 4,
    )(par, b3, r, lm, u, w)
    return untiles(sol), untiles(res)


def solution(mesh):
    in_specs = (
        P("slab", None, "rve", None),
        P("slab", None, "rve", None),
        P("slab", "rve", None),
        P(),
    )
    out_specs = (P("slab", None, "rve", None), P("slab", None, "rve", None))
    return jax.shard_map(sweeps, mesh=mesh, in_specs=in_specs, out_specs=out_specs, check_vma=False)
```

time: 71.6 us -> 34.1 us (0.48)
  other arithmetic: 22.4 us -> 0 us
  Pallas kernels: 0 us -> 11.1 us
  local copies, waits for them, and re-layouts: 11 us -> 0.01 us
  starting transfers between devices: 20.2 us -> 11.9 us
  waiting for transfers between devices: 15.6 us -> 10.1 us
  between operations: 2.22 us -> 0.9 us
    pallas_call x0 -> x9, Pallas kernels: none -> 11.1 us  [the longest x1 3.06 us: sweeps(): call(kernel_last, [SMEM] + [VMEM] * 5, (whole, whole) + state, [sm, st],...]
    slice x121 -> x1, local copies, waits for them, and re-layouts: 10.9 us -> 0.01 us  [sweeps(): b3 = send(a2[2:4], across)]
    ppermute x10 -> x7, starting transfers between devices: 20.2 us -> 11.9 us  [send(): return lax.ppermute(v, 'slab', pairs)]
    add x37 -> x0, other arithmetic: 5.85 us -> none  [the longest x14 2.38 us: plus_next(): return value + jnp.roll(value, -1, axis)]
    ppermute x10 -> x7, waiting for transfers between devices: 15.6 us -> 10.1 us  [send(): return lax.ppermute(v, 'slab', pairs)]
    mul x34 -> x0, other arithmetic: 5.28 us -> none  [the longest x7 2.23 us: element_terms(): 0.25 * (plus_prev(prev_minus(col_x, -2), -1) + plus_prev(prev_minus(col_y...]
    broadcast_in_dim x2 -> x0, other arithmetic: 4.83 us -> none  [on_device(): stacked = jnp.concatenate([load, lame[:, None], shear[:, None]], 1)]
    sub x15 -> x0, other arithmetic: 4.59 us -> none  [the longest x7 2.96 us: prev_minus(): return jnp.roll(value, 1, axis) - value]
  transfers between devices with their start and end apart: 10 -> 7, of which waited for: 6 -> 2; matrix products, arithmetic and copies ran while one was open for 12% -> 0% of each run, Pallas kernels for 0% -> 17%
where the time goes in v1:
time: 34.1 us; the launch traced here: 34 us
  starting transfers between devices  11.9 us (35%)
  Pallas kernels  11.1 us (33%)
  waiting for transfers between devices  10.1 us (30%)
  between operations  0.9 us (3%)
    ppermute x7, starting transfers between devices, send(): return lax.ppermute(v, 'slab', pairs)  11.9 us
    ppermute x7, waiting for transfers between devices, send(): return lax.ppermute(v, 'slab', pairs)  10.1 us
    pallas_call x1, Pallas kernels, sweeps(): call(kernel_last, [SMEM] + [VMEM] * 5, (whole, whole) + state, [sm, st],...  3.06 us
    pallas_call x1, Pallas kernels, sweeps(): call(kernel_mid, [VMEM] * 7, state + (f32(3, 3),), [sm, st], {3: 0, 4: 1,...  1.88 us
    pallas_call x1, Pallas kernels, sweeps(): call(kernel_near, [VMEM] * 5, state, [sm, st], {1: 0, 2: 1, 3: 2, 4: 3}, 11)  1.5 us
    pallas_call x1, Pallas kernels, sweeps(): call(kernel_inner, [VMEM] * 5, state, [sm, st], {1: 0, 2: 1, 3: 2, 4: 3},...  1.36 us
    pallas_call x1, Pallas kernels, sweeps(): call(kernel_prep, [SMEM] + [HBM] * 4, (shape(7), whole, whole, six), [],...  1.22 us
    pallas_call x1, Pallas kernels, sweeps(): call(kernel_lead, [VMEM] * 4, state, [sm, st], {0: 0, 1: 1, 2: 2, 3: 3}, 6)  0.79 us
  transfers between devices with their start and end apart: 7, of which 2 were waited for; matrix products, arithmetic and copies ran while one was open for 0% of the time, Pallas kernels for 17%

profile of v1, /device:TPU:2, one launch (start us, length us, event | category | flops | bytes accessed | tf_op | source)
XLA Modules:
  0.0 34.0 jit_solution(13510649951911104041)
XLA Ops:
  0.6 0.1 collective-permute-start
  0.7 0.5 %collective-permute-start.1 = (s32[4,32,256]{2,1,0:T(8,128)}, s32[4,32,256]{2,1,0:T(8,128)S(1)}, u32[]{:S(2)}, u32[]{:S(2)}) collective-permute-start(s32[4,32,256]{2,1,0:T(8,128)} %param.6), channel_id=1, source_target_pairs={{0,1},{1,0},{2,3},{3,2},{4,5},{5,4},{6,7},{7,6},{8,9},{9,8},{10,11... | collective-permute-start | bytes 393224 | tf_op jit(solution)/shard_map/ppermute | solution.py:412
  1.2 1.2 %shard_map.59 = (f32[7,64,128]{2,1,0:T(8,128)S(1)}, f32[4,3,64,128]{3,2,1,0:T(8,128)S(1)}, f32[4,3,64,128]{3,2,1,0:T(8,128)S(1)}, f32[6,8,256]{2,1,0:T(8,128)S(1)}) custom-call(s32[1]{0:T(128)} %bitcast.par, f32[2,3]{1,0:T(2,128)} %mod_h.1, f32[4,3,64,128]{3,2,1,0:T(8,128)} %bitcast.39, f32[4,3,64,128]{3,2,1,0:T(8,128)} %bitcast.38, s32[4,64,128]{2,1,0:T(8,128)} %bitcast.40), custom_call_target="tpu_custom_call" | custom-call | flops 1400000 | bytes 1000000 | tf_op jit(solution)/shard_map/pallas_call | solution.py:428
  2.5 0.5 %shard_map.60 = (f32[2,13,3,4,8,256]{5,4,3,2,1,0:T(8,128)S(1)}, f32[16,2,4,8,256]{4,3,2,1,0:T(8,128)S(1)}, f32[4,3,4,8,256]{4,3,2,1,0:T(8,128)S(1)}, f32[5,3,4,8,256]{4,3,2,1,0:T(8,128)S(1)}) custom-call(s32[1]{0:T(128)} %bitcast.par, f32[6,8,256]{2,1,0:T(8,128)S(1)} %get-tuple-element.38.mod, f32[4,3,64,128]{3,2,1,0:T(8,128)S(1)} %get-tuple-element.41.u, ...), custom_call_target="tpu_custom_call" | custom-call | flops 2800000 | bytes 2000000 | tf_op jit(solution)/shard_map/pallas_call | solution.py:438
  3.0 0.0 collective-permute-done.1
  3.0 0.0 collective-permute-done
  3.0 0.3 shard_map.61
  3.3 0.2 collective-permute-start.2
  3.5 6.9 %collective-permute-start.4 = (f32[5,3,4,8,256]{4,3,2,1,0:T(8,128)S(1)}, f32[5,3,4,8,256]{4,3,2,1,0:T(8,128)S(1)}, u32[]{:S(2)}, u32[]{:S(2)}) collective-permute-start(f32[5,3,4,8,256]{4,3,2,1,0:T(8,128)S(1)} %get-tuple-element.46), channel_id=1, source_target_pairs={{0,31},{1,2},{2,1},{3,4},{4,3},{5,6},{6,5},{7,8},{8,7},{9,10},{10,... | collective-permute-start | bytes 1474568 | tf_op jit(solution)/shard_map/ppermute | solution.py:412
  10.4 0.0 collective-permute-start.5
  10.4 8.9 %collective-permute-done.5.pb = f32[7,64,128]{2,1,0:T(8,128)S(1)} collective-permute-done((f32[7,64,128]{2,1,0:T(8,128)S(1)}, f32[7,64,128]{2,1,0:T(8,128)S(1)}, u32[]{:S(2)}, u32[]{:S(2)}) %collective-permute-start.5) | collective-permute-done | bytes 229408 | tf_op jit(solution)/shard_map/ppermute | solution.py:412
  19.4 0.4 %shard_map.62 = (f32[2,13,3,4,8,256]{5,4,3,2,1,0:T(8,128)S(1)}, f32[16,2,4,8,256]{4,3,2,1,0:T(8,128)S(1)}, f32[4,3,4,8,256]{4,3,2,1,0:T(8,128)S(1)}, f32[13,4,8,256]{3,2,1,0:T(8,128)S(1)}, f32[3,4,8,256]{3,2,1,0:T(8,128)S(1)}) custom-call(s32[1]{0:T(128)} %bitcast.par, ...), custom_call_target="tpu_custom_call", output_to_operand_aliasing={{0}: (3, {}), {1}: (4, {}), {2}: (5, {})} | custom-call | flops 2800000 | bytes 2000000 | tf_op jit(solution)/shard_map/pallas_call | solution.py:451
  19.8 0.0 collective-permute-done.2.a2
  19.8 1.5 %shard_map.63 = (f32[2,13,3,4,8,256]{5,4,3,2,1,0:T(8,128)S(1)}, f32[16,2,4,8,256]{4,3,2,1,0:T(8,128)S(1)}, f32[4,3,4,8,256]{4,3,2,1,0:T(8,128)S(1)}, f32[13,4,8,256]{3,2,1,0:T(8,128)S(1)}) custom-call(f32[5,3,4,8,256]{4,3,2,1,0:T(8,128)S(1)} %collective-permute-done.2.a2, ...), custom_call_target="tpu_custom_call", output_to_operand_aliasing={{0}: (1, {}), {1}: (2, {}), {2}: (3, {}), {3}: (4, {})} | custom-call | flops 7700000 | bytes 5500000 | tf_op jit(solution)/shard_map/pallas_call | solution.py:459
  21.3 0.0 collective-permute-done.4.b2
  21.3 1.9 %shard_map.64 = (f32[2,13,3,4,8,256]{5,4,3,2,1,0:T(8,128)S(1)}, f32[16,2,4,8,256]{4,3,2,1,0:T(8,128)S(1)}, f32[4,3,4,8,256]{4,3,2,1,0:T(8,128)S(1)}, f32[13,4,8,...) custom-call(f32[6,8,256]{2,1,0:T(8,128)S(1)} %get-tuple-element.38.m, ...), custom_call_target="tpu_custom_call", output_to_operand_aliasing={{0}: (3, {}), {1}: (4, {}), {2}: (5, {}), {3}: (6, {})} | custom-call | flops 9800000 | bytes 7000000 | tf_op jit(solution)/shard_map/pallas_call | solution.py:463
  23.2 0.1 collective-permute-start.6
  23.3 4.1 %collective-permute-start.3 = (f32[2,3,4,8,256]{4,3,2,1,0:T(8,128)S(1)}, f32[2,3,4,8,256]{4,3,2,1,0:T(8,128)S(1)}, u32[]{:S(2)}, u32[]{:S(2)}) collective-permute-start(f32[2,3,4,8,256]{4,3,2,1,0:T(8,128)S(1)} %slice.4), channel_id=1, source_target_pairs={{0,31},{1,2},{2,1},{3,4},{4,3},{5,6},{6,5},{7,8},{8,7},{9,10},{10,... | collective-permute-start | bytes 589832 | tf_op jit(solution)/shard_map/ppermute | solution.py:412
  27.4 0.8 %shard_map.65 = (f32[2,13,3,4,8,256]{5,4,3,2,1,0:T(8,128)S(1)}, f32[16,2,4,8,256]{4,3,2,1,0:T(8,128)S(1)}, f32[4,3,4,8,256]{4,3,2,1,0:T(8,128)S(1)}, f32[13,4,8,256]{3,2,1,0:T(8,128)S(1)}) custom-call(f32[2,13,3,4,8,256]{5,4,3,2,1,0:T(8,128)S(1)} %get-tuple-element.60.r_in, ...), custom_call_target="tpu_custom_call", output_to_operand_aliasing={{0}: (0, {}), {1}: (1, {}), {2}: (2, {}), {3}: (3, {})} | custom-call | flops 4200000 | bytes 3000000 | tf_op jit(solution)/shard_map/pallas_call | solution.py:467
  28.2 0.0 collective-permute-done.6.a3
  28.3 1.4 %shard_map.66 = (f32[2,13,3,4,8,256]{5,4,3,2,1,0:T(8,128)S(1)}, f32[16,2,4,8,256]{4,3,2,1,0:T(8,128)S(1)}, f32[4,3,4,8,256]{4,3,2,1,0:T(8,128)S(1)}, f32[13,4,8,256]{3,2,1,0:T(8,128)S(1)}) custom-call(f32[3,3,4,8,256]{4,3,2,1,0:T(8,128)S(1)} %collective-permute-done.6.a3, ...), custom_call_target="tpu_custom_call", output_to_operand_aliasing={{0}: (1, {}), {1}: (2, {}), {2}: (3, {}), {3}: (4, {})} | custom-call | flops 7000000 | bytes 5000000 | tf_op jit(solution)/shard_map/pallas_call | solution.py:470
  29.6 1.2 %collective-permute-done.3.b3 = f32[2,3,4,8,256]{4,3,2,1,0:T(8,128)S(1)} collective-permute-done((f32[2,3,4,8,256]{4,3,2,1,0:T(8,128)S(1)}, f32[2,3,4,8,256]{4,3,2,1,0:T(8,128)S(1)}, u32[]{:S(2)}, u32[]{:S(2)}) %collective-permute-start.3) | collective-permute-done | bytes 196640 | tf_op jit(solution)/shard_map/ppermute | solution.py:412
  30.8 3.1 %shard_map.67 = (f32[4,3,64,128]{3,2,1,0:T(8,128)}, f32[4,3,64,128]{3,2,1,0:T(8,128)}, f32[2,13,3,4,8,256]{5,4,3,2,1,0:T(8,128)S(1)}, f32[16,2,4,8,256]{4,3,2,1,...) custom-call(s32[1]{0:T(128)} %bitcast.par, ...), custom_call_target="tpu_custom_call", output_to_operand_aliasing={{2}: (2, {}), {3}: (3, {}), {4}: (4, {}), {5}: (5, {})} | custom-call | flops 12600000 | bytes 9000000 | tf_op jit(solution)/shard_map/pallas_call | solution.py:473
  (1 shorter events, 0.0 us)
Async XLA Ops:
  0.6 2.4 %collective-permute-start = (f32[4,3,32,256]{3,2,1,0:T(8,128)}, f32[4,3,32,256]{3,2,1,0:T(8,128)S(1)}, u32[]{:S(2)}, u32[]{:S(2)}) collective-permute-start(f32[4,3,32,256]{3,2,1,0:T(8,128)} %param.4), channel_id=1, source_target_pairs={{0,1},{1,0},{2,3},{3,2},{4,5},{5,4},{6,7},{7,6},{8,9},{9,8},{10,11... | collective-permute-start | bytes 1179656 | tf_op jit(solution)/shard_map/ppermute | solution.py:412
  0.7 2.2 %collective-permute-start.1 = (s32[4,32,256]{2,1,0:T(8,128)}, s32[4,32,256]{2,1,0:T(8,128)S(1)}, u32[]{:S(2)}, u32[]{:S(2)}) collective-permute-start(s32[4,32,256]{2,1,0:T(8,128)} %param.6), channel_id=1, source_target_pairs={{0,1},{1,0},{2,3},{3,2},{4,5},{5,4},{6,7},{7,6},{8,9},{9,8},{10,11... | collective-permute-start | bytes 393224 | tf_op jit(solution)/shard_map/ppermute | solution.py:412
  3.3 16.5 %collective-permute-start.2 = (f32[5,3,4,8,256]{4,3,2,1,0:T(8,128)S(1)}, f32[5,3,4,8,256]{4,3,2,1,0:T(8,128)S(1)}, u32[]{:S(2)}, u32[]{:S(2)}) collective-permute-start(f32[5,3,4,8,256]{4,3,2,1,0:T(8,128)S(1)} %get-tuple-element.46), channel_id=1, source_target_pairs={{0,1},{1,0},{2,3},{3,2},{4,5},{5,4},{6,7},{7,6},{8,9},{9,8},{10,11... | collective-permute-start | bytes 1474568 | tf_op jit(solution)/shard_map/ppermute | solution.py:412
  3.5 17.8 %collective-permute-start.4 = (f32[5,3,4,8,256]{4,3,2,1,0:T(8,128)S(1)}, f32[5,3,4,8,256]{4,3,2,1,0:T(8,128)S(1)}, u32[]{:S(2)}, u32[]{:S(2)}) collective-permute-start(f32[5,3,4,8,256]{4,3,2,1,0:T(8,128)S(1)} %get-tuple-element.46), channel_id=1, source_target_pairs={{0,31},{1,2},{2,1},{3,4},{4,3},{5,6},{6,5},{7,8},{8,7},{9,10},{10,... | collective-permute-start | bytes 1474568 | tf_op jit(solution)/shard_map/ppermute | solution.py:412
  10.4 9.0 %collective-permute-start.5 = (f32[7,64,128]{2,1,0:T(8,128)S(1)}, f32[7,64,128]{2,1,0:T(8,128)S(1)}, u32[]{:S(2)}, u32[]{:S(2)}) collective-permute-start(f32[7,64,128]{2,1,0:T(8,128)S(1)} %get-tuple-element.40.own), channel_id=1, source_target_pairs={{0,31},{1,2},{2,1},{3,4},{4,3},{5,6},{6,5},{7,8},{8,7},{9,10},{10,... | collective-permute-start | bytes 688136 | tf_op jit(solution)/shard_map/ppermute | solution.py:412
  23.2 5.0 %collective-permute-start.6 = (f32[3,3,4,8,256]{4,3,2,1,0:T(8,128)S(1)}, f32[3,3,4,8,256]{4,3,2,1,0:T(8,128)S(1)}, u32[]{:S(2)}, u32[]{:S(2)}) collective-permute-start(f32[3,3,4,8,256]{4,3,2,1,0:T(8,128)S(1)} %get-tuple-element.59), channel_id=1, source_target_pairs={{0,1},{1,0},{2,3},{3,2},{4,5},{5,4},{6,7},{7,6},{8,9},{9,8},{10,11... | collective-permute-start | bytes 884744 | tf_op jit(solution)/shard_map/ppermute | solution.py:412
  23.3 7.5 %collective-permute-start.3 = (f32[2,3,4,8,256]{4,3,2,1,0:T(8,128)S(1)}, f32[2,3,4,8,256]{4,3,2,1,0:T(8,128)S(1)}, u32[]{:S(2)}, u32[]{:S(2)}) collective-permute-start(f32[2,3,4,8,256]{4,3,2,1,0:T(8,128)S(1)} %slice.4), channel_id=1, source_target_pairs={{0,31},{1,2},{2,1},{3,4},{4,3},{5,6},{6,5},{7,8},{8,7},{9,10},{10,... | collective-permute-start | bytes 589832 | tf_op jit(solution)/shard_map/ppermute | solution.py:412

commit v2 on v1

v2 whole, which is shorter than its diff:
```python
import jax
import jax.numpy as jnp
from jax import lax
from jax.experimental import pallas as pl
from jax.experimental.pallas import tpu as pltpu
from jax.sharding import PartitionSpec as P


OWN = 4
DEPTH = 6
INNER = 3
NODES = DEPTH + OWN + INNER
LAYERS = 16
N0 = DEPTH
L0 = 8

VMEM = pl.BlockSpec(memory_space=pltpu.VMEM)
SMEM = pl.BlockSpec(memory_space=pltpu.SMEM)
HBM = pl.BlockSpec(memory_space=pltpu.HBM)
ROW = (4, 8, 256)


def f32(*shape):
    return jax.ShapeDtypeStruct(shape + ROW, jnp.float32)


def even_rows():
    return lax.broadcasted_iota(jnp.int32, (8, 128), 0) % 2 == 0


def load_raw(ref, index, r):
    a = ref[index + (pl.ds(r, 8, stride=8), slice(None))]
    b = ref[index + (pl.ds(r + 4, 8, stride=8), slice(None))]
    even = even_rows()
    low = jnp.where(even, a, pltpu.roll(b, 1, 0))
    high = jnp.where(even, pltpu.roll(a, 7, 0), b)
    return jnp.concatenate([low, high], axis=1)


def store_raw(ref, index, r, value):
    low, high = value[:, :128], value[:, 128:]
    even = even_rows()
    ref[index + (pl.ds(r, 8, stride=8), slice(None))] = jnp.where(even, low, pltpu.roll(high, 1, 0))
    ref[index + (pl.ds(r + 4, 8, stride=8), slice(None))] = jnp.where(even, pltpu.roll(low, 7, 0), high)


def y_next(v):
    return pltpu.roll(v, 255, 1)


def y_prev(v):
    return pltpu.roll(v, 1, 1)


def x_prev(rows, r):
    return rows[r - 1] if r > 0 else pltpu.roll(rows[3], 1, 0)


def y_stage(sm, get, m):
    for c in range(3):
        for r in range(4):
            d = get(m, c, r)
            n = y_next(d)
            sm[m + L0, c, r] = d + n
            sm[m + L0, 3 + c, r] = n - d


def stress_step(sm, st, lm, m, get, save=None):
    first = prev = None

    def stress(z, nxt, r):
        x0, y1, z2, _, _, e, pd, qd = z
        gxx = nxt[0] - x0
        gyy = nxt[1] + y1
        gzz = nxt[2] + z2
        lame, mu = lm[m + L0, 0, r], lm[m + L0, 1, r]
        lt = lame * (gxx + gyy + gzz)
        mu2 = mu + mu
        values = (
            lt + mu2 * gxx,
            mu * (nxt[3] + pd),
            lt + mu2 * gyy,
            mu * (nxt[4] + qd),
            mu * (nxt[5] + e),
            lt + mu2 * gzz,
        )
        for i, v in enumerate(values):
            st[m + L0, i, r] = v
            if save is not None:
                save[i, r] = v

    for r in range(4):
        s, my, j = [], [], []
        for c in range(3):
            d = get(m + 1, c, r)
            n = y_next(d)
            su, mu_ = d + n, n - d
            sl, ml = sm[m + L0, c, r], sm[m + L0, 3 + c, r]
            sm[m + 1 + L0, c, r] = su
            sm[m + 1 + L0, 3 + c, r] = mu_
            s.append(sl + su)
            my.append(ml + mu_)
            j.append(su - sl)
        z = (s[0], my[1], j[2], my[0] + s[1], j[0] + s[2], j[1] + my[2], my[0] - s[1], j[0] - s[2])
        if r == 0:
            first = z
        else:
            stress(prev, z, r - 1)
        prev = z
    stress(prev, tuple(pltpu.roll(v, 7, 0) for v in first[:6]), 3)


def node_sums(st, m, r, above, below, top):
    upper = st.at[m + L0] if top is None else top
    new = [upper[i, r] if above else None for i in range(6)]
    old = [st[m - 1 + L0, i, r] if below else None for i in range(6)]

    def plus(i):
        return new[i] if not below else old[i] if not above else new[i] + old[i]

    def minus(i):
        return -new[i] if not below else old[i] if not above else old[i] - new[i]

    xx, xy, yy, xz, yz = (plus(i) for i in range(5))
    dxz, dyz, dzz = (minus(i) for i in range(3, 6))
    return (
        (xx + dxz, xy + dyz, xz + dzz),
        (dxz - xx, dyz - xy, dzz - xz),
        (xy, yy, yz),
    )


def node_step(st, m, finish, above=True, below=True, top=None):
    first = prev = None

    def out(pq, pp, ph, r):
        for c in range(3):
            g = pp[c] + pq[1][c]
            hh = ph[c] + pq[2][c]
            finish(m, c, r, (g - hh) + y_prev(g + hh))

    for r in range(4):
        pq = node_sums(st, m, r, above, below, top)
        if r == 0:
            first = pq
        else:
            out(pq, prev[0], prev[2], r)
        prev = pq
    roll = lambda v: pltpu.roll(v, 1, 0)
    out(first, tuple(map(roll, prev[0])), tuple(map(roll, prev[2])), 0)


def advance(refs, s, lo, hi, save=None, top=None):
    R, W, LM, U, sm, st = refs
    src, dst = s % 2, (s + 1) % 2

    def get(m, c, r):
        return W[m + N0, r] * R[src, m + N0, c, r]

    def finisher(own):
        def finish(m, c, r, k):
            old = R[src, m + N0, c, r]
            R[dst, m + N0, c, r] = old - k
            if own:
                U[m, c, r] = U[m, c, r] + W[m + N0, r] * old

        return finish

    def layer(m):
        if m < hi or (m == hi and top is None):
            stress_step(sm, st, LM, m, get)

    y_stage(sm, get, lo - 1)
    stress_step(sm, st, LM, lo - 1, get, save)
    layer(lo)
    for m in range(lo, hi + 1):
        layer(m + 1)
        node_step(st, m, finisher(0 <= m < OWN), top=top if m == hi else None)


def materials(LM, mod, load, m):
    for r in range(4):
        v = load(r)
        one, two = v == 1, v == 2
        for i in range(2):
            LM[m + L0, i, r] = jnp.where(two, mod[3 * i + 2], jnp.where(one, mod[3 * i + 1], mod[3 * i]))


def raw(ref, k):
    return lambda r: load_raw(ref, (k,), r)


def weights(W, LM, lo, hi):
    for m in range(lo, hi + 1):
        t = []
        for r in range(4):
            v = (LM[m - 1 + L0, 0, r] + LM[m + L0, 0, r]) + 4.0 * (LM[m - 1 + L0, 1, r] + LM[m + L0, 1, r])
            t.append(v)
        for r in range(4):
            v = t[r] + x_prev(t, r)
            W[m + N0, r] = 0.5 / (v + y_prev(v))


def sign_of(par):
    return (1 - 2 * par[0]).astype(jnp.float32)


def oriented(v, c, sign):
    return v * sign if c == 2 else v


def kernel_own(par, mod_h, u_h, f_h, ph_h, R, LM, U, PA, B1, MOD, F3, sm, st, u, f, ph, mod, sem):
    odd, sign = par[0], sign_of(par)
    copies = [
        pltpu.make_async_copy(src, dst, sem.at[i])
        for i, (src, dst) in enumerate(((mod_h, mod), (ph_h, ph), (u_h, u), (f_h, f)))
    ]
    for copy in copies:
        copy.start()
    plane = lambda m: jnp.where(odd == 1, 3 - m, m)
    copies[0].wait()
    for i in range(2):
        for j in range(3):
            MOD[3 * i + j] = jnp.full((8, 256), mod[i, j] * 0.0625, jnp.float32)
    copies[1].wait()
    for k in range(4):
        for r in range(4):
            B1[3 + k, r] = load_raw(ph, (k,), r).astype(jnp.float32)
        materials(LM, MOD, lambda r: B1[3 + k, r], jnp.where(odd == 1, 2 - k, k))
    copies[2].wait()
    for m in range(4):
        for c in range(3):
            for r in range(4):
                v = oriented(load_raw(u, (plane(m), c), r), c, sign)
                U[m, c, r] = v
                if m == 0:
                    B1[c, r] = v

    def get(m, c, r):
        return U[m, c, r]

    def finish(m, c, r, k):
        v = oriented(load_raw(f, (plane(m), c), r), c, sign) - k
        R[0, m + N0, c, r] = v
        B1[7 + 3 * m + c, r] = v
        if m > 0:
            PA[m - 1, c, r] = v

    y_stage(sm, get, 0)
    stress_step(sm, st, LM, 0, get)
    stress_step(sm, st, LM, 1, get)
    copies[3].wait()
    for c in range(3):
        for r in range(4):
            F3[c, r] = oriented(load_raw(f, (plane(3), c), r), c, sign)
    node_step(st, 0, finish, below=False)
    stress_step(sm, st, LM, 2, get)
    node_step(st, 1, finish)
    node_step(st, 2, finish)


def kernel_rest(par, mod, f3, b1, ua, pa, r_in, lm_in, u_in, p_in, R, LM, U, PA, P3, uw, sm, st):
    odd, sign = par[0], sign_of(par)
    for k in range(4):
        materials(LM, mod, raw(pa, k), jnp.where(odd == 1, 6 - k, 4 + k))
    for c in range(3):
        for r in range(4):
            uw[0, c, r] = oriented(load_raw(ua, (3 * odd, c), r), c, sign)
    for j in range(3):
        for r in range(4):
            v = load_raw(pa, (jnp.where(odd == 1, 3 - j, max(j - 1, 0)),), r).astype(jnp.float32)
            P3[3, j, r] = jnp.where(odd == 1, v, b1[6, r]) if j == 0 else v

    def get(m, c, r):
        return U[m, c, r] if m < 4 else uw[0, c, r]

    def finish(m, c, r, k):
        v = f3[c, r] - k
        R[0, m + N0, c, r] = v
        PA[2, c, r] = v
        P3[0, c, r] = v

    y_stage(sm, get, 2)
    stress_step(sm, st, LM, 2, get)
    stress_step(sm, st, LM, 3, get)
    node_step(st, 3, finish)


def flipped(v, c):
    return -v if c == 2 else v


def kernel_pack(a2, p_in, P3):
    for j in range(2):
        for c in range(3):
            P3[1 + j, c] = flipped(a2[2 - j, c], c)


def kernel_near(a2, r_in, lm_in, u_in, R, LM, U, W, EN, sm, st):
    for j in range(3):
        for c in range(3):
            R[0, 4 + j + N0, c] = flipped(a2[2 - j, c], c)
    weights(W, LM, 1, 6)
    refs = (R, W, LM, U, sm, st)
    advance(refs, 0, 2, 5, EN.at[0])
    advance(refs, 1, 3, 4, EN.at[1])


def kernel_mid(par, mod, b1, en, r_in, lm_in, u_in, w_in, R, LM, U, W, ES, PAY, edge, sm, st):
    odd = par[0]
    for k in range(4):
        materials(LM, mod, lambda r: b1[3 + k, r], jnp.where(odd == 1, -2 - k, k - 4))
    weights(W, LM, -3, 0)

    def get(m, c, r):
        return flipped(b1[c, r], c) if m == -1 else U[0, c, r]

    def keep(m, c, r, k):
        edge[c, r] = k

    def take(m, c, r, k):
        R[0, N0, c, r] = R[0, N0, c, r] - k

    y_stage(sm, get, -1)
    stress_step(sm, st, LM, -1, get)
    node_step(st, -1, keep, below=False)
    node_step(st, 0, take, above=False)
    for j in range(3):
        for c in range(3):
            for r in range(4):
                v = flipped(b1[7 + 3 * j + c, r], c)
                R[0, -1 - j + N0, c, r] = v - edge[c, r] if j == 0 else v
    refs = (R, W, LM, U, sm, st)
    advance(refs, 0, -2, 1, ES.at[0], en.at[0])
    advance(refs, 1, -1, 2, ES.at[1], en.at[1])
    advance(refs, 2, 0, 3, ES.at[2])
    for j in range(3):
        for c in range(3):
            PAY[j, c] = R[1, 1 + j + N0, c]


def kernel_lead(r_in, lm_in, u_in, w_in, e_in, R, LM, U, W, ES, sm, st):
    advance((R, W, LM, U, sm, st), 3, 1, 2, ES.at[3])


def kernel_inner(a3, r_in, lm_in, u_in, w_in, e_in, R, LM, U, W, ES, sm, st):
    for j in range(3):
        for c in range(3):
            R[1, 4 + j + N0, c] = flipped(a3[2 - j, c], c)
    refs = (R, W, LM, U, sm, st)
    advance(refs, 3, 3, 5)
    advance(refs, 4, 2, 4, ES.at[4])
    advance(refs, 5, 3, 3, ES.at[5])


def kernel_last(par, mod, b3, es, r_in, lm_in, u_in, w_in, sol_h, res_h, R, LM, U, W, sm, st, sol, res, sem):
    odd, sign = par[0], sign_of(par)

    def put(m):
        k = jnp.where(odd == 1, 3 - m, m)
        for c in range(3):
            for r in range(4):
                store_raw(sol, (m, c), r, oriented(U[m, c, r], c, sign))
                store_raw(res, (m, c), r, oriented(R[0, m + N0, c, r], c, sign))
        copies = [
            pltpu.make_async_copy(src.at[m], dst.at[k], sem.at[2 * m + i])
            for i, (src, dst) in enumerate(((sol, sol_h), (res, res_h)))
        ]
        for copy in copies:
            copy.start()
        return copies

    started = put(3)
    for j in range(3):
        materials(LM, mod, lambda r: b3[3, j, r], -5 - j)
    weights(W, LM, -6, -4)
    for j in range(3):
        for c in range(3):
            R[0, -4 - j + N0, c] = flipped(b3[j, c], c)
    refs = (R, W, LM, U, sm, st)
    advance(refs, 0, -5, -3, top=es.at[0])
    advance(refs, 1, -4, -2, top=es.at[1])
    advance(refs, 2, -3, -1, top=es.at[2])
    advance(refs, 3, -2, 0, top=es.at[3])
    advance(refs, 4, -1, 1, top=es.at[4])
    advance(refs, 5, 0, 2, top=es.at[5])
    for m in range(3):
        started = started + put(m)
    for copy in started:
        copy.wait()


def call(kernel, in_specs, out_shape, scratch, alias, planes, extra=(), out_specs=None):
    return pl.pallas_call(
        kernel,
        out_shape=out_shape,
        in_specs=in_specs,
        out_specs=out_specs or tuple(VMEM for _ in out_shape),
        scratch_shapes=[pltpu.VMEM(s + ROW, jnp.float32) for s in scratch] + list(extra),
        input_output_aliases=alias,
        compiler_params=pltpu.CompilerParams(vmem_limit_bytes=14 << 20),
        cost_estimate=pl.CostEstimate(flops=planes * 700000, bytes_accessed=planes * 500000, transcendentals=0),
    )


def tiles(x):
    lead = x.shape[:-2]
    return x.reshape(lead + (4, 8, 2, 128)).swapaxes(-3, -2).reshape(lead + (64, 128))


def untiles(x):
    lead = x.shape[:-2]
    return x.reshape(lead + (4, 2, 8, 128)).swapaxes(-3, -2).reshape(lead + (32, 256))


def sweeps(displacement, load, phase, moduli):
    count = lax.axis_size("slab")
    odd = lax.bitwise_and(lax.axis_index("slab"), 1)
    par = odd.reshape(1).astype(jnp.int32)
    inside = [(i, i ^ 1) for i in range(count)]
    across = [(i, (i - 1) % count if i % 2 == 0 else (i + 1) % count) for i in range(count)]

    def send(v, pairs):
        return lax.ppermute(v, "slab", pairs)

    sm, st = (LAYERS, 6), (LAYERS, 6)
    R, LM, U, W = f32(2, NODES, 3), f32(LAYERS, 2), f32(OWN, 3), f32(NODES)
    state = (R, LM, U, W)
    dma = lambda n: pltpu.SemaphoreType.DMA((n,))
    block = lambda n, kind=jnp.float32: pltpu.VMEM((n, 64, 128), kind)
    in_hbm = lambda v: pltpu.with_memory_space_constraint(v, pltpu.HBM)
    u_t, f_t, ph_t = (in_hbm(tiles(v)) for v in (displacement, load, phase))
    moduli = in_hbm(moduli)

    whole = jax.ShapeDtypeStruct((OWN, 3, 64, 128), jnp.float32)
    six = jax.ShapeDtypeStruct((6, 8, 256), jnp.float32)
    fields = pltpu.VMEM((OWN, 3, 64, 128), jnp.float32)
    ua = send(displacement, inside)
    pa = send(phase, inside)
    r, lm, u, pay, pay1, mod, f3 = call(
        kernel_own,
        [SMEM] + [HBM] * 4,
        (R, LM, U, f32(3, 3), f32(16), six, f32(3)),
        [sm, st],
        {},
        4,
        [fields, fields, block(4, jnp.int32), pltpu.SMEM((2, 3), jnp.float32), dma(4)],
    )(par, moduli, u_t, f_t, ph_t)
    b1 = send(pay1, across)
    r, lm, u, pay, pay3 = call(
        kernel_rest,
        [SMEM] + [VMEM] * 9,
        (R, LM, U, f32(3, 3), f32(4, 3)),
        [(1, 3), sm, st],
        {6: 0, 7: 1, 8: 2, 9: 3},
        2,
    )(par, mod, f3, pay1, tiles(ua), tiles(pa), r, lm, u, pay)
    a2 = send(pay, inside)
    (pay3,) = call(kernel_pack, [VMEM] * 2, (f32(4, 3),), [], {1: 0}, 1)(a2, pay3)
    b3 = send(pay3, across)
    r, lm, u, w, en = call(
        kernel_near, [VMEM] * 4, state + (f32(2, 6),), [sm, st], {1: 0, 2: 1, 3: 2}, 8
    )(a2, r, lm, u)
    r, lm, u, w, es, pay = call(
        kernel_mid,
        [SMEM] + [VMEM] * 7,
        state + (f32(6, 6), f32(3, 3)),
        [(3,), sm, st],
        {4: 0, 5: 1, 6: 2, 7: 3},
        14,
    )(par, mod, b1, en, r, lm, u, w)
    a3 = send(pay, inside)
    r, lm, u, w, es = call(
        kernel_lead, [VMEM] * 5, state + (f32(6, 6),), [sm, st], {0: 0, 1: 1, 2: 2, 3: 3, 4: 4}, 3
    )(r, lm, u, w, es)
    r, lm, u, w, es = call(
        kernel_inner, [VMEM] * 6, state + (f32(6, 6),), [sm, st], {1: 0, 2: 1, 3: 2, 4: 3, 5: 4}, 9
    )(a3, r, lm, u, w, es)
    sol, res, _, _, _, _ = call(
        kernel_last,
        [SMEM] + [VMEM] * 7,
        (whole, whole) + state,
        [sm, st],
        {4: 2, 5: 3, 6: 4, 7: 5},
        24,
        [fields, fields, dma(8)],
        (HBM, HBM) + (VMEM,) * 4,
    )(par, mod, b3, es, r, lm, u, w)
    return untiles(sol), untiles(res)


def solution(mesh):
    in_specs = (
        P("slab", None, "rve", None),
        P("slab", None, "rve", None),
        P("slab", "rve", None),
        P(),
    )
    out_specs = (P("slab", None, "rve", None), P("slab", None, "rve", None))
    return jax.shard_map(sweeps, mesh=mesh, in_specs=in_specs, out_specs=out_specs, check_vma=False)
```

time: 34.1 us -> 25.7 us (0.75)
  starting transfers between devices: 11.9 us -> 8.32 us
  waiting for transfers between devices: 10.1 us -> 6.66 us
  Pallas kernels: 11.1 us -> 9.87 us
    ppermute x7 -> x6, starting transfers between devices: 11.9 us -> 8.32 us  [send(): return lax.ppermute(v, 'slab', pairs)]
    ppermute x7 -> x6, waiting for transfers between devices: 10.1 us -> 6.66 us  [send(): return lax.ppermute(v, 'slab', pairs)]
    pallas_call x9 -> x8, Pallas kernels: 11.1 us -> 9.87 us  [the longest x1 3.23 us: sweeps(): call(kernel_last, [SMEM] + [VMEM] * 7, (whole, whole) + state, [sm, st],...]
  transfers between devices with their start and end apart: 7 -> 6, of which waited for: 2 -> 5; matrix products, arithmetic and copies ran while one was open for 0% -> 0% of each run, Pallas kernels for 17% -> 26%
where the time goes in v2:
time: 25.7 us; the launch traced here: 25.6 us
  Pallas kernels  9.87 us (38%)
  starting transfers between devices  8.32 us (32%)
  waiting for transfers between devices  6.66 us (26%)
  between operations  0.7 us (3%)
    ppermute x6, starting transfers between devices, send(): return lax.ppermute(v, 'slab', pairs)  8.32 us
    ppermute x6, waiting for transfers between devices, send(): return lax.ppermute(v, 'slab', pairs)  6.66 us
    pallas_call x1, Pallas kernels, sweeps(): call(kernel_last, [SMEM] + [VMEM] * 7, (whole, whole) + state, [sm, st],...  3.23 us
    pallas_call x1, Pallas kernels, sweeps(): call(kernel_mid, [SMEM] + [VMEM] * 7, state + (f32(6, 6), f32(3, 3)), [(3...  2.02 us
    pallas_call x1, Pallas kernels, sweeps(): call(kernel_own, [SMEM] + [HBM] * 4, (R, LM, U, f32(3, 3), f32(16), six,...  1.58 us
    pallas_call x1, Pallas kernels, sweeps(): call(kernel_inner, [VMEM] * 6, state + (f32(6, 6),), [sm, st], {1: 0, 2:...  1.26 us
    pallas_call x1, Pallas kernels, sweeps(): call(kernel_near, [VMEM] * 4, state + (f32(2, 6),), [sm, st], {1: 0, 2: 1...  1.08 us
  transfers between devices with their start and end apart: 6, of which 5 were waited for; matrix products, arithmetic and copies ran while one was open for 0% of the time, Pallas kernels for 26%

profile of v2, /device:TPU:2, one launch (start us, length us, event | category | flops | bytes accessed | tf_op | source)
XLA Modules:
  0.0 25.6 jit_solution(7588931337355775067)
XLA Ops:
  0.6 0.1 collective-permute-start
  0.7 1.6 %shard_map.59 = (f32[2,13,3,4,8,256]{5,4,3,2,1,0:T(8,128)S(1)}, f32[16,2,4,8,256]{4,3,2,1,0:T(8,128)S(1)}, f32[4,3,4,8,256]{4,3,2,1,0:T(8,128)S(1)}, f32[3,3,4,8...) custom-call(s32[1]{0:T(128)} %bitcast.par, ...), custom_call_target="tpu_custom_call" | custom-call | flops 2800000 | bytes 2000000 | tf_op jit(solution)/shard_map/pallas_call | solution.py:440
  2.3 7.0 %collective-permute-start.4 = (f32[16,4,8,256]{3,2,1,0:T(8,128)S(1)}, f32[16,4,8,256]{3,2,1,0:T(8,128)S(1)}, u32[]{:S(2)}, u32[]{:S(2)}) collective-permute-start(f32[16,4,8,256]{3,2,1,0:T(8,128)S(1)} %get-tuple-element.39.b1), channel_id=1, source_target_pairs={{0,31},{1,2},{2,1},{3,4},{4,3},{5,6},{6,5},{7,8},{8,7},{9,10},{10,... | collective-permute-start | bytes 1572872 | tf_op jit(solution)/shard_map/ppermute | solution.py:424
  9.4 0.0 collective-permute-start.1
  9.4 1.6 %collective-permute-done.1 = s32[4,32,256]{2,1,0:T(8,128)S(1)} collective-permute-done((s32[4,32,256]{2,1,0:T(8,128)}, s32[4,32,256]{2,1,0:T(8,128)S(1)}, u32[]{:S(2)}, u32[]{:S(2)}) %collective-permute-start.1) | collective-permute-done | bytes 131104 | tf_op jit(solution)/shard_map/ppermute | solution.py:424
  10.9 0.0 collective-permute-done
  10.9 0.3 %shard_map.60 = (f32[2,13,3,4,8,256]{5,4,3,2,1,0:T(8,128)S(1)}, f32[16,2,4,8,256]{4,3,2,1,0:T(8,128)S(1)}, f32[4,3,4,8,256]{4,3,2,1,0:T(8,128)S(1)}, f32[3,3,4,8...) custom-call(s32[1]{0:T(128)} %bitcast.par, ...), custom_call_target="tpu_custom_call", output_to_operand_aliasing={{0}: (6, {}), {1}: (7, {}), {2}: (8, {}), {3}: (9, {})} | custom-call | flops 1400000 | bytes 1000000 | tf_op jit(solution)/shard_map/pallas_call | solution.py:450
  11.2 0.2 collective-permute-start.2
  11.5 1.4 %collective-permute-done.2.a2 = f32[3,3,4,8,256]{4,3,2,1,0:T(8,128)S(1)} collective-permute-done((f32[3,3,4,8,256]{4,3,2,1,0:T(8,128)S(1)}, f32[3,3,4,8,256]{4,3,2,1,0:T(8,128)S(1)}, u32[]{:S(2)}, u32[]{:S(2)}) %collective-permute-start.2) | collective-permute-done | bytes 294944 | tf_op jit(solution)/shard_map/ppermute | solution.py:424
  12.9 0.8 %collective-permute-start.3 = (f32[4,3,4,8,256]{4,3,2,1,0:T(8,128)S(1)}, f32[4,3,4,8,256]{4,3,2,1,0:T(8,128)S(1)}, u32[]{:S(2)}, u32[]{:S(2)}) collective-permute-start(f32[4,3,4,8,256]{4,3,2,1,0:T(8,128)S(1)} %shard_map.61), channel_id=1, source_target_pairs={{0,31},{1,2},{2,1},{3,4},{4,3},{5,6},{6,5},{7,8},{8,7},{9,10},{10,... | collective-permute-start | bytes 1179656 | tf_op jit(solution)/shard_map/ppermute | solution.py:424
  13.8 1.1 %shard_map.62 = (f32[2,13,3,4,8,256]{5,4,3,2,1,0:T(8,128)S(1)}, f32[16,2,4,8,256]{4,3,2,1,0:T(8,128)S(1)}, f32[4,3,4,8,256]{4,3,2,1,0:T(8,128)S(1)}, f32[13,4,8,...) custom-call(f32[3,3,4,8,256]{4,3,2,1,0:T(8,128)S(1)} %collective-permute-don, ...), custom_call_target="tpu_custom_call", output_to_operand_aliasing={{0}: (1, {}), {1}: (2, {}), {2}: (3, {})} | custom-call | flops 5600000 | bytes 4000000 | tf_op jit(solution)/shard_map/pallas_call | solution.py:461
  14.9 1.4 %collective-permute-done.4.b1 = f32[16,4,8,256]{3,2,1,0:T(8,128)S(1)} collective-permute-done((f32[16,4,8,256]{3,2,1,0:T(8,128)S(1)}, f32[16,4,8,256]{3,2,1,0:T(8,128)S(1)}, u32[]{:S(2)}, u32[]{:S(2)}) %collective-permute-start.4) | collective-permute-done | bytes 524320 | tf_op jit(solution)/shard_map/ppermute | solution.py:424
  16.2 2.0 %shard_map.63 = (f32[2,13,3,4,8,256]{5,4,3,2,1,0:T(8,128)S(1)}, f32[16,2,4,8,256]{4,3,2,1,0:T(8,128)S(1)}, f32[4,3,4,8,256]{4,3,2,1,0:T(8,128)S(1)}, f32[13,4,8,...) custom-call(s32[1]{0:T(128)} %bitcast.par, ...), custom_call_target="tpu_custom_call", output_to_operand_aliasing={{0}: (4, {}), {1}: (5, {}), {2}: (6, {}), {3}: (7, {})} | custom-call | flops 9800000 | bytes 7000000 | tf_op jit(solution)/shard_map/pallas_call | solution.py:464
  18.3 0.1 collective-permute-start.5
  18.4 0.4 %shard_map.64 = (f32[2,13,3,4,8,256]{5,4,3,2,1,0:T(8,128)S(1)}, f32[16,2,4,8,256]{4,3,2,1,0:T(8,128)S(1)}, f32[4,3,4,8,256]{4,3,2,1,0:T(8,128)S(1)}, f32[13,4,8,...) custom-call(f32[2,13,3,4,8,256]{5,4,3,2,1,0:T(8,128)S(1)} %get-tuple, ...), custom_call_target="tpu_custom_call", output_to_operand_aliasing={{0}: (0, {}), {1}: (1, {}), {2}: (2, {}), {3}: (3, {}), {4}... | custom-call | flops 2100000 | bytes 1500000 | tf_op jit(solution)/shard_map/pallas_call | solution.py:473
  18.8 1.2 %collective-permute-done.5.a3 = f32[3,3,4,8,256]{4,3,2,1,0:T(8,128)S(1)} collective-permute-done((f32[3,3,4,8,256]{4,3,2,1,0:T(8,128)S(1)}, f32[3,3,4,8,256]{4,3,2,1,0:T(8,128)S(1)}, u32[]{:S(2)}, u32[]{:S(2)}) %collective-permute-start.5) | collective-permute-done | bytes 294944 | tf_op jit(solution)/shard_map/ppermute | solution.py:424
  19.9 1.3 %shard_map.65 = (f32[2,13,3,4,8,256]{5,4,3,2,1,0:T(8,128)S(1)}, f32[16,2,4,8,256]{4,3,2,1,0:T(8,128)S(1)}, f32[4,3,4,8,256]{4,3,2,1,0:T(8,128)S(1)}, f32[13,4,8,...) custom-call(f32[3,3,4,8,256]{4,3,2,1,0:T(8,128)S(1)} %collective-per, ...), custom_call_target="tpu_custom_call", output_to_operand_aliasing={{0}: (1, {}), {1}: (2, {}), {2}: (3, {}), {3}: (4, {}), {4}... | custom-call | flops 6300000 | bytes 4500000 | tf_op jit(solution)/shard_map/pallas_call | solution.py:476
  21.2 1.1 %collective-permute-done.3.b3 = f32[4,3,4,8,256]{4,3,2,1,0:T(8,128)S(1)} collective-permute-done((f32[4,3,4,8,256]{4,3,2,1,0:T(8,128)S(1)}, f32[4,3,4,8,256]{4,3,2,1,0:T(8,128)S(1)}, u32[]{:S(2)}, u32[]{:S(2)}) %collective-permute-start.3) | collective-permute-done | bytes 393248 | tf_op jit(solution)/shard_map/ppermute | solution.py:424
  22.3 3.2 %shard_map.66 = (f32[4,3,64,128]{3,2,1,0:T(8,128)}, f32[4,3,64,128]{3,2,1,0:T(8,128)}, f32[2,13,3,4,8,256]{5,4,3,2,1,0:T(8,128)S(1)}, f32[16,2,4,8,256]{4,3,2,1,...) custom-call(s32[1]{0:T(128)} %bitcast.par, ...), custom_call_target="tpu_custom_call", output_to_operand_aliasing={{2}: (4, {}), {3}: (5, {}), {4}: (6, {}), {5}: (7, {})} | custom-call | flops 16800000 | bytes 12000000 | tf_op jit(solution)/shard_map/pallas_call | solution.py:479
  (1 shorter events, 0.0 us)
Async XLA Ops:
  0.6 10.3 %collective-permute-start = (f32[4,3,32,256]{3,2,1,0:T(8,128)}, f32[4,3,32,256]{3,2,1,0:T(8,128)S(1)}, u32[]{:S(2)}, u32[]{:S(2)}) collective-permute-start(f32[4,3,32,256]{3,2,1,0:T(8,128)} %param.4), channel_id=1, source_target_pairs={{0,1},{1,0},{2,3},{3,2},{4,5},{5,4},{6,7},{7,6},{8,9},{9,8},{10,11... | collective-permute-start | bytes 1179656 | tf_op jit(solution)/shard_map/ppermute | solution.py:424
  2.3 13.9 %collective-permute-start.4 = (f32[16,4,8,256]{3,2,1,0:T(8,128)S(1)}, f32[16,4,8,256]{3,2,1,0:T(8,128)S(1)}, u32[]{:S(2)}, u32[]{:S(2)}) collective-permute-start(f32[16,4,8,256]{3,2,1,0:T(8,128)S(1)} %get-tuple-element.39.b1), channel_id=1, source_target_pairs={{0,31},{1,2},{2,1},{3,4},{4,3},{5,6},{6,5},{7,8},{8,7},{9,10},{10,... | collective-permute-start | bytes 1572872 | tf_op jit(solution)/shard_map/ppermute | solution.py:424
  9.4 1.6 %collective-permute-start.1 = (s32[4,32,256]{2,1,0:T(8,128)}, s32[4,32,256]{2,1,0:T(8,128)S(1)}, u32[]{:S(2)}, u32[]{:S(2)}) collective-permute-start(s32[4,32,256]{2,1,0:T(8,128)} %param.6), channel_id=1, source_target_pairs={{0,1},{1,0},{2,3},{3,2},{4,5},{5,4},{6,7},{7,6},{8,9},{9,8},{10,11... | collective-permute-start | bytes 393224 | tf_op jit(solution)/shard_map/ppermute | solution.py:424
  11.2 1.7 %collective-permute-start.2 = (f32[3,3,4,8,256]{4,3,2,1,0:T(8,128)S(1)}, f32[3,3,4,8,256]{4,3,2,1,0:T(8,128)S(1)}, u32[]{:S(2)}, u32[]{:S(2)}) collective-permute-start(f32[3,3,4,8,256]{4,3,2,1,0:T(8,128)S(1)} %get-tuple-element.44), channel_id=1, source_target_pairs={{0,1},{1,0},{2,3},{3,2},{4,5},{5,4},{6,7},{7,6},{8,9},{9,8},{10,11... | collective-permute-start | bytes 884744 | tf_op jit(solution)/shard_map/ppermute | solution.py:424
  12.9 9.4 %collective-permute-start.3 = (f32[4,3,4,8,256]{4,3,2,1,0:T(8,128)S(1)}, f32[4,3,4,8,256]{4,3,2,1,0:T(8,128)S(1)}, u32[]{:S(2)}, u32[]{:S(2)}) collective-permute-start(f32[4,3,4,8,256]{4,3,2,1,0:T(8,128)S(1)} %shard_map.61), channel_id=1, source_target_pairs={{0,31},{1,2},{2,1},{3,4},{4,3},{5,6},{6,5},{7,8},{8,7},{9,10},{10,... | collective-permute-start | bytes 1179656 | tf_op jit(solution)/shard_map/ppermute | solution.py:424
  18.3 1.7 %collective-permute-start.5 = (f32[3,3,4,8,256]{4,3,2,1,0:T(8,128)S(1)}, f32[3,3,4,8,256]{4,3,2,1,0:T(8,128)S(1)}, u32[]{:S(2)}, u32[]{:S(2)}) collective-permute-start(f32[3,3,4,8,256]{4,3,2,1,0:T(8,128)S(1)} %get-tuple-element.54), channel_id=1, source_target_pairs={{0,1},{1,0},{2,3},{3,2},{4,5},{5,4},{6,7},{7,6},{8,9},{9,8},{10,11... | collective-permute-start | bytes 884744 | tf_op jit(solution)/shard_map/ppermute | solution.py:424

commit v3 on v2

--- a/solution.py
+++ b/solution.py
@@ -150,7 +150,7 @@
     out(first, tuple(map(roll, prev[0])), tuple(map(roll, prev[2])), 0)
 
 
-def advance(refs, s, lo, hi, save=None, top=None):
+def advance(refs, s, lo, hi, save=None, top=None, after=None):
     R, W, LM, U, sm, st = refs
     src, dst = s % 2, (s + 1) % 2
 
@@ -161,7 +161,7 @@
         def finish(m, c, r, k):
             old = R[src, m + N0, c, r]
             R[dst, m + N0, c, r] = old - k
-            if own:
+            if own and after is None:
                 U[m, c, r] = U[m, c, r] + W[m + N0, r] * old
 
         return finish
@@ -176,6 +176,8 @@
     for m in range(lo, hi + 1):
         layer(m + 1)
         node_step(st, m, finisher(0 <= m < OWN), top=top if m == hi else None)
+        if after is not None:
+            after(m)
 
 
 def materials(LM, mod, load, m):
@@ -184,10 +186,6 @@
         one, two = v == 1, v == 2
         for i in range(2):
             LM[m + L0, i, r] = jnp.where(two, mod[3 * i + 2], jnp.where(one, mod[3 * i + 1], mod[3 * i]))
-
-
-def raw(ref, k):
-    return lambda r: load_raw(ref, (k,), r)
 
 
 def weights(W, LM, lo, hi):
@@ -209,7 +207,11 @@
     return v * sign if c == 2 else v
 
 
-def kernel_own(par, mod_h, u_h, f_h, ph_h, R, LM, U, PA, B1, MOD, F3, sm, st, u, f, ph, mod, sem):
+def flipped(v, c):
+    return -v if c == 2 else v
+
+
+def kernel_own(par, mod_h, u_h, f_h, ph_h, R, LM, U, A1, B1, MOD, sm, st, u, f, ph, mod, sem):
     odd, sign = par[0], sign_of(par)
     copies = [
         pltpu.make_async_copy(src, dst, sem.at[i])
@@ -225,7 +227,9 @@
     copies[1].wait()
     for k in range(4):
         for r in range(4):
-            B1[3 + k, r] = load_raw(ph, (k,), r).astype(jnp.float32)
+            v = load_raw(ph, (k,), r).astype(jnp.float32)
+            A1[3 + k, r] = v
+            B1[3 + k, r] = v
         materials(LM, MOD, lambda r: B1[3 + k, r], jnp.where(odd == 1, 2 - k, k))
     copies[2].wait()
     for m in range(4):
@@ -235,6 +239,8 @@
                 U[m, c, r] = v
                 if m == 0:
                     B1[c, r] = v
+                if m == 3:
+                    A1[c, r] = v
 
     def get(m, c, r):
         return U[m, c, r]
@@ -242,71 +248,57 @@
     def finish(m, c, r, k):
         v = oriented(load_raw(f, (plane(m), c), r), c, sign) - k
         R[0, m + N0, c, r] = v
-        B1[7 + 3 * m + c, r] = v
+        if m < 3:
+            B1[7 + 3 * m + c, r] = v
         if m > 0:
-            PA[m - 1, c, r] = v
+            A1[7 + 3 * (3 - m) + c, r] = v
 
     y_stage(sm, get, 0)
     stress_step(sm, st, LM, 0, get)
     stress_step(sm, st, LM, 1, get)
     copies[3].wait()
-    for c in range(3):
-        for r in range(4):
-            F3[c, r] = oriented(load_raw(f, (plane(3), c), r), c, sign)
     node_step(st, 0, finish, below=False)
     stress_step(sm, st, LM, 2, get)
-    node_step(st, 1, finish)
-    node_step(st, 2, finish)
-
-
-def kernel_rest(par, mod, f3, b1, ua, pa, r_in, lm_in, u_in, p_in, R, LM, U, PA, P3, uw, sm, st):
-    odd, sign = par[0], sign_of(par)
+    for m in range(1, 4):
+        node_step(st, m, finish, above=m < 3)
+
+
+def kernel_fin(par, mod, b1, a1, r_in, lm_in, u_in, R, LM, U, P3, sm, st):
+    odd = par[0]
     for k in range(4):
-        materials(LM, mod, raw(pa, k), jnp.where(odd == 1, 6 - k, 4 + k))
+        materials(LM, mod, lambda r: a1[3 + k, r], jnp.where(odd == 1, 6 - k, 4 + k))
+    for j in range(3):
+        for r in range(4):
+            v = a1[3 + jnp.where(odd == 1, 3 - j, max(j - 1, 0)), r]
+            P3[3, j, r] = jnp.where(odd == 1, v, b1[6, r]) if j == 0 else v
     for c in range(3):
-        for r in range(4):
-            uw[0, c, r] = oriented(load_raw(ua, (3 * odd, c), r), c, sign)
-    for j in range(3):
-        for r in range(4):
-            v = load_raw(pa, (jnp.where(odd == 1, 3 - j, max(j - 1, 0)),), r).astype(jnp.float32)
-            P3[3, j, r] = jnp.where(odd == 1, v, b1[6, r]) if j == 0 else v
+        v = flipped(a1[10 + c], c)
+        R[0, 5 + N0, c] = v
+        P3[2, c] = v
+        R[0, 6 + N0, c] = flipped(a1[13 + c], c)
 
     def get(m, c, r):
-        return U[m, c, r] if m < 4 else uw[0, c, r]
+        return U[3, c, r] if m == 3 else flipped(a1[c, r], c)
 
     def finish(m, c, r, k):
-        v = f3[c, r] - k
+        v = (R[0, 3 + N0, c, r] if m == 3 else flipped(a1[7 + c, r], c)) - k
         R[0, m + N0, c, r] = v
-        PA[2, c, r] = v
-        P3[0, c, r] = v
-
-    y_stage(sm, get, 2)
-    stress_step(sm, st, LM, 2, get)
+        P3[m - 3, c, r] = v
+
+    y_stage(sm, get, 3)
     stress_step(sm, st, LM, 3, get)
-    node_step(st, 3, finish)
-
-
-def flipped(v, c):
-    return -v if c == 2 else v
-
-
-def kernel_pack(a2, p_in, P3):
-    for j in range(2):
-        for c in range(3):
-            P3[1 + j, c] = flipped(a2[2 - j, c], c)
-
-
-def kernel_near(a2, r_in, lm_in, u_in, R, LM, U, W, EN, sm, st):
-    for j in range(3):
-        for c in range(3):
-            R[0, 4 + j + N0, c] = flipped(a2[2 - j, c], c)
+    node_step(st, 3, finish, below=False)
+    node_step(st, 4, finish, above=False)
+
+
+def kernel_near(r_in, lm_in, u_in, R, LM, U, W, EN, sm, st):
     weights(W, LM, 1, 6)
     refs = (R, W, LM, U, sm, st)
     advance(refs, 0, 2, 5, EN.at[0])
     advance(refs, 1, 3, 4, EN.at[1])
 
 
-def kernel_mid(par, mod, b1, en, r_in, lm_in, u_in, w_in, R, LM, U, W, ES, PAY, edge, sm, st):
+def kernel_mid(par, mod, b1, en, r_in, lm_in, u_in, w_in, R, LM, U, W, E1, PAY, edge, sm, st):
     odd = par[0]
     for k in range(4):
         materials(LM, mod, lambda r: b1[3 + k, r], jnp.where(odd == 1, -2 - k, k - 4))
@@ -331,16 +323,20 @@
                 v = flipped(b1[7 + 3 * j + c, r], c)
                 R[0, -1 - j + N0, c, r] = v - edge[c, r] if j == 0 else v
     refs = (R, W, LM, U, sm, st)
-    advance(refs, 0, -2, 1, ES.at[0], en.at[0])
-    advance(refs, 1, -1, 2, ES.at[1], en.at[1])
-    advance(refs, 2, 0, 3, ES.at[2])
+    advance(refs, 0, -1, 1, E1.at[0], en.at[0])
+    advance(refs, 1, 0, 2, E1.at[1], en.at[1])
+    advance(refs, 2, 1, 3, E1.at[2])
     for j in range(3):
         for c in range(3):
             PAY[j, c] = R[1, 1 + j + N0, c]
 
 
-def kernel_lead(r_in, lm_in, u_in, w_in, e_in, R, LM, U, W, ES, sm, st):
-    advance((R, W, LM, U, sm, st), 3, 1, 2, ES.at[3])
+def kernel_lead(e1, r_in, lm_in, u_in, w_in, R, LM, U, W, ES, sm, st):
+    refs = (R, W, LM, U, sm, st)
+    advance(refs, 0, -2, -2, ES.at[0], e1.at[0])
+    advance(refs, 1, -1, -1, ES.at[1], e1.at[1])
+    advance(refs, 2, 0, 0, ES.at[2], e1.at[2])
+    advance(refs, 3, 1, 2, ES.at[3])
 
 
 def kernel_inner(a3, r_in, lm_in, u_in, w_in, e_in, R, LM, U, W, ES, sm, st):
@@ -355,22 +351,21 @@
 
 def kernel_last(par, mod, b3, es, r_in, lm_in, u_in, w_in, sol_h, res_h, R, LM, U, W, sm, st, sol, res, sem):
     odd, sign = par[0], sign_of(par)
-
-    def put(m):
-        k = jnp.where(odd == 1, 3 - m, m)
+    started = []
+
+    def put(buf, dst, i, m, get):
         for c in range(3):
             for r in range(4):
-                store_raw(sol, (m, c), r, oriented(U[m, c, r], c, sign))
-                store_raw(res, (m, c), r, oriented(R[0, m + N0, c, r], c, sign))
-        copies = [
-            pltpu.make_async_copy(src.at[m], dst.at[k], sem.at[2 * m + i])
-            for i, (src, dst) in enumerate(((sol, sol_h), (res, res_h)))
-        ]
-        for copy in copies:
-            copy.start()
-        return copies
-
-    started = put(3)
+                store_raw(buf, (m, c), r, oriented(get(c, r), c, sign))
+        copy = pltpu.make_async_copy(buf.at[m], dst.at[jnp.where(odd == 1, 3 - m, m)], sem.at[2 * m + i])
+        copy.start()
+        started.append(copy)
+
+    def put_res(m):
+        put(res, res_h, 1, m, lambda c, r: R[0, m + N0, c, r])
+
+    put(sol, sol_h, 0, 3, lambda c, r: U[3, c, r])
+    put_res(3)
     for j in range(3):
         materials(LM, mod, lambda r: b3[3, j, r], -5 - j)
     weights(W, LM, -6, -4)
@@ -378,14 +373,11 @@
         for c in range(3):
             R[0, -4 - j + N0, c] = flipped(b3[j, c], c)
     refs = (R, W, LM, U, sm, st)
-    advance(refs, 0, -5, -3, top=es.at[0])
-    advance(refs, 1, -4, -2, top=es.at[1])
-    advance(refs, 2, -3, -1, top=es.at[2])
-    advance(refs, 3, -2, 0, top=es.at[3])
-    advance(refs, 4, -1, 1, top=es.at[4])
-    advance(refs, 5, 0, 2, top=es.at[5])
+    for s in range(5):
+        advance(refs, s, s - 5, s - 3, top=es.at[s])
     for m in range(3):
-        started = started + put(m)
+        put(sol, sol_h, 0, m, lambda c, r: U[m, c, r] + W[m + N0, r] * R[1, m + N0, c, r])
+    advance(refs, 5, 0, 2, top=es.at[5], after=put_res)
     for copy in started:
         copy.wait()
 
@@ -435,44 +427,36 @@
     whole = jax.ShapeDtypeStruct((OWN, 3, 64, 128), jnp.float32)
     six = jax.ShapeDtypeStruct((6, 8, 256), jnp.float32)
     fields = pltpu.VMEM((OWN, 3, 64, 128), jnp.float32)
-    ua = send(displacement, inside)
-    pa = send(phase, inside)
-    r, lm, u, pay, pay1, mod, f3 = call(
+    r, lm, u, pay, pay1, mod = call(
         kernel_own,
         [SMEM] + [HBM] * 4,
-        (R, LM, U, f32(3, 3), f32(16), six, f32(3)),
+        (R, LM, U, f32(16), f32(16), six),
         [sm, st],
         {},
         4,
         [fields, fields, block(4, jnp.int32), pltpu.SMEM((2, 3), jnp.float32), dma(4)],
     )(par, moduli, u_t, f_t, ph_t)
     b1 = send(pay1, across)
-    r, lm, u, pay, pay3 = call(
-        kernel_rest,
-        [SMEM] + [VMEM] * 9,
-        (R, LM, U, f32(3, 3), f32(4, 3)),
-        [(1, 3), sm, st],
-        {6: 0, 7: 1, 8: 2, 9: 3},
-        2,
-    )(par, mod, f3, pay1, tiles(ua), tiles(pa), r, lm, u, pay)
-    a2 = send(pay, inside)
-    (pay3,) = call(kernel_pack, [VMEM] * 2, (f32(4, 3),), [], {1: 0}, 1)(a2, pay3)
+    a1 = send(pay, inside)
+    r, lm, u, pay3 = call(
+        kernel_fin, [SMEM] + [VMEM] * 6, (R, LM, U, f32(4, 3)), [sm, st], {4: 0, 5: 1, 6: 2}, 2
+    )(par, mod, pay1, a1, r, lm, u)
     b3 = send(pay3, across)
     r, lm, u, w, en = call(
-        kernel_near, [VMEM] * 4, state + (f32(2, 6),), [sm, st], {1: 0, 2: 1, 3: 2}, 8
-    )(a2, r, lm, u)
-    r, lm, u, w, es, pay = call(
+        kernel_near, [VMEM] * 3, state + (f32(2, 6),), [sm, st], {0: 0, 1: 1, 2: 2}, 8
+    )(r, lm, u)
+    r, lm, u, w, e1, pay = call(
         kernel_mid,
         [SMEM] + [VMEM] * 7,
-        state + (f32(6, 6), f32(3, 3)),
+        state + (f32(3, 6), f32(3, 3)),
         [(3,), sm, st],
         {4: 0, 5: 1, 6: 2, 7: 3},
         14,
     )(par, mod, b1, en, r, lm, u, w)
     a3 = send(pay, inside)
     r, lm, u, w, es = call(
-        kernel_lead, [VMEM] * 5, state + (f32(6, 6),), [sm, st], {0: 0, 1: 1, 2: 2, 3: 3, 4: 4}, 3
-    )(r, lm, u, w, es)
+        kernel_lead, [VMEM] * 5, state + (f32(6, 6),), [sm, st], {1: 0, 2: 1, 3: 2, 4: 3}, 6
+    )(e1, r, lm, u, w)
     r, lm, u, w, es = call(
         kernel_inner, [VMEM] * 6, state + (f32(6, 6),), [sm, st], {1: 0, 2: 1, 3: 2, 4: 3, 5: 4}, 9
     )(a3, r, lm, u, w, es)

time: 25.7 us -> 25.3 us (0.984)
  the two profiles are of different devices: /device:TPU:2 before, /device:TPU:1 now
where the time goes in v3:
time: 25.3 us; the launch traced here: 25.2 us
  Pallas kernels  10.2 us (40%)
  waiting for transfers between devices  7.44 us (29%)
  starting transfers between devices  6.91 us (27%)
  between operations  0.68 us (3%)
    ppermute x4, waiting for transfers between devices, send(): return lax.ppermute(v, 'slab', pairs)  7.44 us
    ppermute x4, starting transfers between devices, send(): return lax.ppermute(v, 'slab', pairs)  6.91 us
    pallas_call x1, Pallas kernels, sweeps(): call(kernel_last, [SMEM] + [VMEM] * 7, (whole, whole) + state, [sm, st],...  3.28 us
    pallas_call x1, Pallas kernels, sweeps(): call(kernel_mid, [SMEM] + [VMEM] * 7, state + (f32(3, 6), f32(3, 3)), [(3...  1.65 us
    pallas_call x1, Pallas kernels, sweeps(): call(kernel_own, [SMEM] + [HBM] * 4, (R, LM, U, f32(16), f32(16), six), [...  1.63 us
    pallas_call x1, Pallas kernels, sweeps(): call(kernel_inner, [VMEM] * 6, state + (f32(6, 6),), [sm, st], {1: 0, 2:...  1.27 us
    pallas_call x1, Pallas kernels, sweeps(): call(kernel_near, [VMEM] * 3, state + (f32(2, 6),), [sm, st], {0: 0, 1: 1...  1.07 us
    pallas_call x1, Pallas kernels, sweeps(): call(kernel_lead, [VMEM] * 5, state + (f32(6, 6),), [sm, st], {1: 0, 2: 1...  1.02 us
  transfers between devices with their start and end apart: 4, of which 3 were waited for; matrix products, arithmetic and copies ran while one was open for 0% of the time, Pallas kernels for 21%

profile of v3, /device:TPU:1, one launch (start us, length us, event | category | flops | bytes accessed | tf_op | source)
XLA Modules:
  0.0 25.2 jit_solution(15930836909267809857)
XLA Ops:
  0.6 1.6 %shard_map.59 = (f32[2,13,3,4,8,256]{5,4,3,2,1,0:T(8,128)S(1)}, f32[16,2,4,8,256]{4,3,2,1,0:T(8,128)S(1)}, f32[4,3,4,8,256]{4,3,2,1,0:T(8,128)S(1)}, f32[16,4,8,...) custom-call(s32[1]{0:T(128)} %bitcast.par, f32[2,3]{1,0:T(2,128)} %mod_h.1, ...), custom_call_target="tpu_custom_call" | custom-call | flops 2800000 | bytes 2000000 | tf_op jit(solution)/shard_map/pallas_call | solution.py:430
  2.3 3.3 %collective-permute-start = (f32[16,4,8,256]{3,2,1,0:T(8,128)S(1)}, f32[16,4,8,256]{3,2,1,0:T(8,128)S(1)}, u32[]{:S(2)}, u32[]{:S(2)}) collective-permute-start(f32[16,4,8,256]{3,2,1,0:T(8,128)S(1)} %get-tuple-element.37), channel_id=1, source_target_pairs={{0,1},{1,0},{2,3},{3,2},{4,5},{5,4},{6,7},{7,6},{8,9},{9,8},{10,11... | collective-permute-start | bytes 1572872 | tf_op jit(solution)/shard_map/ppermute | solution.py:416
  5.6 0.0 collective-permute-start.2
  5.6 1.5 %collective-permute-done.a1 = f32[16,4,8,256]{3,2,1,0:T(8,128)S(1)} collective-permute-done((f32[16,4,8,256]{3,2,1,0:T(8,128)S(1)}, f32[16,4,8,256]{3,2,1,0:T(8,128)S(1)}, u32[]{:S(2)}, u32[]{:S(2)}) %collective-permute-start) | collective-permute-done | bytes 524320 | tf_op jit(solution)/shard_map/ppermute | solution.py:416
  7.1 0.3 %shard_map.60 = (f32[2,13,3,4,8,256]{5,4,3,2,1,0:T(8,128)S(1)}, f32[16,2,4,8,256]{4,3,2,1,0:T(8,128)S(1)}, f32[4,3,4,8,256]{4,3,2,1,0:T(8,128)S(1)}, f32[4,3,4,8,256]{4,3,2,1,0:T(8,128)S(1)}) custom-call(s32[1]{0:T(128)} %bitcast.par, f32[6,8,256]{2,1,0:T(8,128)S(1)} %get-tuple-element.35.mod, ...), custom_call_target="tpu_custom_call", output_to_operand_aliasing={{0}: (4, {}), {1}: (5, {}), {2}: (6, {})} | custom-call | flops 1400000 | bytes 1000000 | tf_op jit(solution)/shard_map/pallas_call | solution.py:441
  7.4 0.3 %collective-permute-start.1 = (f32[4,3,4,8,256]{4,3,2,1,0:T(8,128)S(1)}, f32[4,3,4,8,256]{4,3,2,1,0:T(8,128)S(1)}, u32[]{:S(2)}, u32[]{:S(2)}) collective-permute-start(f32[4,3,4,8,256]{4,3,2,1,0:T(8,128)S(1)} %get-tuple-element.41), channel_id=1, source_target_pairs={{0,31},{1,2},{2,1},{3,4},{4,3},{5,6},{6,5},{7,8},{8,7},{9,10},{10,... | collective-permute-start | bytes 1179656 | tf_op jit(solution)/shard_map/ppermute | solution.py:416
  7.7 1.1 %shard_map.61 = (f32[2,13,3,4,8,256]{5,4,3,2,1,0:T(8,128)S(1)}, f32[16,2,4,8,256]{4,3,2,1,0:T(8,128)S(1)}, f32[4,3,4,8,256]{4,3,2,1,0:T(8,128)S(1)}, f32[13,4,8,...) custom-call(f32[2,13,3,4,8,256]{5,4,3,2,1,0:T(8,128)S(1)} %get-tuple-element, ...), custom_call_target="tpu_custom_call", output_to_operand_aliasing={{0}: (0, {}), {1}: (1, {}), {2}: (2, {})} | custom-call | flops 5600000 | bytes 4000000 | tf_op jit(solution)/shard_map/pallas_call | solution.py:445
  8.7 5.7 %collective-permute-done.2.b1 = f32[16,4,8,256]{3,2,1,0:T(8,128)S(1)} collective-permute-done((f32[16,4,8,256]{3,2,1,0:T(8,128)S(1)}, f32[16,4,8,256]{3,2,1,0:T(8,128)S(1)}, u32[]{:S(2)}, u32[]{:S(2)}) %collective-permute-start.2) | collective-permute-done | bytes 524320 | tf_op jit(solution)/shard_map/ppermute | solution.py:416
  14.5 1.7 %shard_map.62 = (f32[2,13,3,4,8,256]{5,4,3,2,1,0:T(8,128)S(1)}, f32[16,2,4,8,256]{4,3,2,1,0:T(8,128)S(1)}, f32[4,3,4,8,256]{4,3,2,1,0:T(8,128)S(1)}, f32[13,4,8,...) custom-call(s32[1]{0:T(128)} %bitcast.par, ...), custom_call_target="tpu_custom_call", output_to_operand_aliasing={{0}: (4, {}), {1}: (5, {}), {2}: (6, {}), {3}: (7, {})} | custom-call | flops 9800000 | bytes 7000000 | tf_op jit(solution)/shard_map/pallas_call | solution.py:448
  16.1 3.3 %collective-permute-start.3 = (f32[3,3,4,8,256]{4,3,2,1,0:T(8,128)S(1)}, f32[3,3,4,8,256]{4,3,2,1,0:T(8,128)S(1)}, u32[]{:S(2)}, u32[]{:S(2)}) collective-permute-start(f32[3,3,4,8,256]{4,3,2,1,0:T(8,128)S(1)} %get-tuple-element.50), channel_id=1, source_target_pairs={{0,1},{1,0},{2,3},{3,2},{4,5},{5,4},{6,7},{7,6},{8,9},{9,8},{10,11... | collective-permute-start | bytes 884744 | tf_op jit(solution)/shard_map/ppermute | solution.py:416
  19.4 1.0 %shard_map.63 = (f32[2,13,3,4,8,256]{5,4,3,2,1,0:T(8,128)S(1)}, f32[16,2,4,8,256]{4,3,2,1,0:T(8,128)S(1)}, f32[4,3,4,8,256]{4,3,2,1,0:T(8,128)S(1)}, f32[13,4,8,...) custom-call(f32[3,6,4,8,256]{4,3,2,1,0:T(8,128)S(1)} %get-tuple-elem, ...), custom_call_target="tpu_custom_call", output_to_operand_aliasing={{0}: (1, {}), {1}: (2, {}), {2}: (3, {}), {3}: (4, {})} | custom-call | flops 4200000 | bytes 3000000 | tf_op jit(solution)/shard_map/pallas_call | solution.py:457
  20.5 0.2 collective-permute-done.3.a3
  20.7 1.3 %shard_map.64 = (f32[2,13,3,4,8,256]{5,4,3,2,1,0:T(8,128)S(1)}, f32[16,2,4,8,256]{4,3,2,1,0:T(8,128)S(1)}, f32[4,3,4,8,256]{4,3,2,1,0:T(8,128)S(1)}, f32[13,4,8,...) custom-call(f32[3,3,4,8,256]{4,3,2,1,0:T(8,128)S(1)} %collective-per, ...), custom_call_target="tpu_custom_call", output_to_operand_aliasing={{0}: (1, {}), {1}: (2, {}), {2}: (3, {}), {3}: (4, {}), {4}... | custom-call | flops 6300000 | bytes 4500000 | tf_op jit(solution)/shard_map/pallas_call | solution.py:460
  21.9 0.0 collective-permute-done.1.b3
  21.9 3.3 %shard_map.65 = (f32[4,3,64,128]{3,2,1,0:T(8,128)}, f32[4,3,64,128]{3,2,1,0:T(8,128)}, f32[2,13,3,4,8,256]{5,4,3,2,1,0:T(8,128)S(1)}, f32[16,2,4,8,256]{4,3,2,1,...) custom-call(s32[1]{0:T(128)} %bitcast.par, ...), custom_call_target="tpu_custom_call", output_to_operand_aliasing={{2}: (4, {}), {3}: (5, {}), {4}: (6, {}), {5}: (7, {})} | custom-call | flops 16800000 | bytes 12000000 | tf_op jit(solution)/shard_map/pallas_call | solution.py:463
Async XLA Ops:
  2.3 4.8 %collective-permute-start = (f32[16,4,8,256]{3,2,1,0:T(8,128)S(1)}, f32[16,4,8,256]{3,2,1,0:T(8,128)S(1)}, u32[]{:S(2)}, u32[]{:S(2)}) collective-permute-start(f32[16,4,8,256]{3,2,1,0:T(8,128)S(1)} %get-tuple-element.37), channel_id=1, source_target_pairs={{0,1},{1,0},{2,3},{3,2},{4,5},{5,4},{6,7},{7,6},{8,9},{9,8},{10,11... | collective-permute-start | bytes 1572872 | tf_op jit(solution)/shard_map/ppermute | solution.py:416
  5.6 8.9 %collective-permute-start.2 = (f32[16,4,8,256]{3,2,1,0:T(8,128)S(1)}, f32[16,4,8,256]{3,2,1,0:T(8,128)S(1)}, u32[]{:S(2)}, u32[]{:S(2)}) collective-permute-start(f32[16,4,8,256]{3,2,1,0:T(8,128)S(1)} %get-tuple-element.36.b1), channel_id=1, source_target_pairs={{0,31},{1,2},{2,1},{3,4},{4,3},{5,6},{6,5},{7,8},{8,7},{9,10},{10,... | collective-permute-start | bytes 1572872 | tf_op jit(solution)/shard_map/ppermute | solution.py:416
  7.4 14.6 %collective-permute-start.1 = (f32[4,3,4,8,256]{4,3,2,1,0:T(8,128)S(1)}, f32[4,3,4,8,256]{4,3,2,1,0:T(8,128)S(1)}, u32[]{:S(2)}, u32[]{:S(2)}) collective-permute-start(f32[4,3,4,8,256]{4,3,2,1,0:T(8,128)S(1)} %get-tuple-element.41), channel_id=1, source_target_pairs={{0,31},{1,2},{2,1},{3,4},{4,3},{5,6},{6,5},{7,8},{8,7},{9,10},{10,... | collective-permute-start | bytes 1179656 | tf_op jit(solution)/shard_map/ppermute | solution.py:416
  16.1 4.5 %collective-permute-start.3 = (f32[3,3,4,8,256]{4,3,2,1,0:T(8,128)S(1)}, f32[3,3,4,8,256]{4,3,2,1,0:T(8,128)S(1)}, u32[]{:S(2)}, u32[]{:S(2)}) collective-permute-start(f32[3,3,4,8,256]{4,3,2,1,0:T(8,128)S(1)} %get-tuple-element.50), channel_id=1, source_target_pairs={{0,1},{1,0},{2,3},{3,2},{4,5},{5,4},{6,7},{7,6},{8,9},{9,8},{10,11... | collective-permute-start | bytes 884744 | tf_op jit(solution)/shard_map/ppermute | solution.py:416

commit v4 on v3

--- a/solution.py
+++ b/solution.py
@@ -211,7 +211,7 @@
     return -v if c == 2 else v
 
 
-def kernel_own(par, mod_h, u_h, f_h, ph_h, R, LM, U, A1, B1, MOD, sm, st, u, f, ph, mod, sem):
+def kernel_own(par, mod_h, u_h, f_h, ph_h, R, LM, U, A1, B1, MOD, sm, st, W, u, f, ph, mod, sem):
     odd, sign = par[0], sign_of(par)
     copies = [
         pltpu.make_async_copy(src, dst, sem.at[i])
@@ -229,8 +229,10 @@
         for r in range(4):
             v = load_raw(ph, (k,), r).astype(jnp.float32)
             A1[3 + k, r] = v
-            B1[3 + k, r] = v
-        materials(LM, MOD, lambda r: B1[3 + k, r], jnp.where(odd == 1, 2 - k, k))
+        materials(LM, MOD, lambda r: A1[3 + k, r], jnp.where(odd == 1, 2 - k, k))
+    for j in range(3):
+        B1[3 + j] = A1[3 + jnp.where(odd == 1, 3 - j, j)]
+    weights(W, LM, 2, 2)
     copies[2].wait()
     for m in range(4):
         for c in range(3):
@@ -249,7 +251,7 @@
         v = oriented(load_raw(f, (plane(m), c), r), c, sign) - k
         R[0, m + N0, c, r] = v
         if m < 3:
-            B1[7 + 3 * m + c, r] = v
+            B1[6 + 3 * m + c, r] = v if m < 2 else W[2 + N0, r] * v
         if m > 0:
             A1[7 + 3 * (3 - m) + c, r] = v
 
@@ -263,18 +265,19 @@
         node_step(st, m, finish, above=m < 3)
 
 
-def kernel_fin(par, mod, b1, a1, r_in, lm_in, u_in, R, LM, U, P3, sm, st):
+def kernel_fin(par, mod, own, a1, r_in, lm_in, u_in, R, LM, U, P3, sm, st):
     odd = par[0]
     for k in range(4):
         materials(LM, mod, lambda r: a1[3 + k, r], jnp.where(odd == 1, 6 - k, 4 + k))
+    P3[9] = own[3 + jnp.where(odd == 1, 0, 2)]
     for j in range(3):
         for r in range(4):
             v = a1[3 + jnp.where(odd == 1, 3 - j, max(j - 1, 0)), r]
-            P3[3, j, r] = jnp.where(odd == 1, v, b1[6, r]) if j == 0 else v
+            P3[10 + j, r] = jnp.where(odd == 1, v, own[6, r]) if j == 0 else v
     for c in range(3):
         v = flipped(a1[10 + c], c)
         R[0, 5 + N0, c] = v
-        P3[2, c] = v
+        P3[6 + c] = v
         R[0, 6 + N0, c] = flipped(a1[13 + c], c)
 
     def get(m, c, r):
@@ -283,7 +286,7 @@
     def finish(m, c, r, k):
         v = (R[0, 3 + N0, c, r] if m == 3 else flipped(a1[7 + c, r], c)) - k
         R[0, m + N0, c, r] = v
-        P3[m - 3, c, r] = v
+        P3[3 * (m - 3) + c, r] = v
 
     y_stage(sm, get, 3)
     stress_step(sm, st, LM, 3, get)
@@ -300,9 +303,10 @@
 
 def kernel_mid(par, mod, b1, en, r_in, lm_in, u_in, w_in, R, LM, U, W, E1, PAY, edge, sm, st):
     odd = par[0]
-    for k in range(4):
-        materials(LM, mod, lambda r: b1[3 + k, r], jnp.where(odd == 1, -2 - k, k - 4))
-    weights(W, LM, -3, 0)
+    for j in range(3):
+        materials(LM, mod, lambda r: b1[3 + j, r], jnp.where(odd == 1, -2 - j, -1 - j))
+    weights(W, LM, -2, 0)
+    W[-3 + N0] = jnp.ones(ROW, jnp.float32)
 
     def get(m, c, r):
         return flipped(b1[c, r], c) if m == -1 else U[0, c, r]
@@ -320,7 +324,7 @@
     for j in range(3):
         for c in range(3):
             for r in range(4):
-                v = flipped(b1[7 + 3 * j + c, r], c)
+                v = flipped(b1[6 + 3 * j + c, r], c)
                 R[0, -1 - j + N0, c, r] = v - edge[c, r] if j == 0 else v
     refs = (R, W, LM, U, sm, st)
     advance(refs, 0, -1, 1, E1.at[0], en.at[0])
@@ -366,12 +370,13 @@
 
     put(sol, sol_h, 0, 3, lambda c, r: U[3, c, r])
     put_res(3)
-    for j in range(3):
-        materials(LM, mod, lambda r: b3[3, j, r], -5 - j)
-    weights(W, LM, -6, -4)
-    for j in range(3):
-        for c in range(3):
-            R[0, -4 - j + N0, c] = flipped(b3[j, c], c)
+    for j in range(4):
+        materials(LM, mod, lambda r: b3[9 + j, r], -4 - j)
+    weights(W, LM, -6, -3)
+    for c in range(3):
+        R[0, -3 + N0, c] = R[0, -3 + N0, c] / W[-3 + N0]
+        for j in range(3):
+            R[0, -4 - j + N0, c] = flipped(b3[3 * j + c], c)
     refs = (R, W, LM, U, sm, st)
     for s in range(5):
         advance(refs, s, s - 5, s - 3, top=es.at[s])
@@ -430,8 +435,8 @@
     r, lm, u, pay, pay1, mod = call(
         kernel_own,
         [SMEM] + [HBM] * 4,
-        (R, LM, U, f32(16), f32(16), six),
-        [sm, st],
+        (R, LM, U, f32(16), f32(15), six),
+        [sm, st, (NODES,)],
         {},
         4,
         [fields, fields, block(4, jnp.int32), pltpu.SMEM((2, 3), jnp.float32), dma(4)],
@@ -439,8 +444,8 @@
     b1 = send(pay1, across)
     a1 = send(pay, inside)
     r, lm, u, pay3 = call(
-        kernel_fin, [SMEM] + [VMEM] * 6, (R, LM, U, f32(4, 3)), [sm, st], {4: 0, 5: 1, 6: 2}, 2
-    )(par, mod, pay1, a1, r, lm, u)
+        kernel_fin, [SMEM] + [VMEM] * 6, (R, LM, U, f32(13)), [sm, st], {4: 0, 5: 1, 6: 2}, 2
+    )(par, mod, pay, a1, r, lm, u)
     b3 = send(pay3, across)
     r, lm, u, w, en = call(
         kernel_near, [VMEM] * 3, state + (f32(2, 6),), [sm, st], {0: 0, 1: 1, 2: 2}, 8

time: 25.3 us -> 25 us (0.988)
  waiting for transfers between devices: 7.44 us -> 7.09 us
    ppermute x4, waiting for transfers between devices: 7.44 us -> 7.09 us  [send(): return lax.ppermute(v, 'slab', pairs)]
where the time goes in v4:
time: 25 us; the launch traced here: 24.9 us
  Pallas kernels  10.2 us (41%)
  waiting for transfers between devices  7.09 us (28%)
  starting transfers between devices  6.91 us (28%)
  between operations  0.68 us (3%)
    ppermute x4, waiting for transfers between devices, send(): return lax.ppermute(v, 'slab', pairs)  7.09 us
    ppermute x4, starting transfers between devices, send(): return lax.ppermute(v, 'slab', pairs)  6.91 us
    pallas_call x1, Pallas kernels, sweeps(): call(kernel_last, [SMEM] + [VMEM] * 7, (whole, whole) + state, [sm, st],...  3.29 us
    pallas_call x1, Pallas kernels, sweeps(): call(kernel_mid, [SMEM] + [VMEM] * 7, state + (f32(3, 6), f32(3, 3)), [(3...  1.66 us
    pallas_call x1, Pallas kernels, sweeps(): call(kernel_own, [SMEM] + [HBM] * 4, (R, LM, U, f32(16), f32(15), six), [...  1.63 us
    pallas_call x1, Pallas kernels, sweeps(): call(kernel_inner, [VMEM] * 6, state + (f32(6, 6),), [sm, st], {1: 0, 2:...  1.27 us
    pallas_call x1, Pallas kernels, sweeps(): call(kernel_near, [VMEM] * 3, state + (f32(2, 6),), [sm, st], {0: 0, 1: 1...  1.07 us
    pallas_call x1, Pallas kernels, sweeps(): call(kernel_lead, [VMEM] * 5, state + (f32(6, 6),), [sm, st], {1: 0, 2: 1...  1.02 us
  transfers between devices with their start and end apart: 4, of which 3 were waited for; matrix products, arithmetic and copies ran while one was open for 0% of the time, Pallas kernels for 21%

profile of v4, /device:TPU:1, one launch (start us, length us, event | category | flops | bytes accessed | tf_op | source)
XLA Modules:
  0.0 24.9 jit_solution(682761144425178708)
XLA Ops:
  0.6 1.6 %shard_map.59 = (f32[2,13,3,4,8,256]{5,4,3,2,1,0:T(8,128)S(1)}, f32[16,2,4,8,256]{4,3,2,1,0:T(8,128)S(1)}, f32[4,3,4,8,256]{4,3,2,1,0:T(8,128)S(1)}, f32[16,4,8,...) custom-call(s32[1]{0:T(128)} %bitcast.par, f32[2,3]{1,0:T(2,128)} %mod_h.1, ...), custom_call_target="tpu_custom_call" | custom-call | flops 2800000 | bytes 2000000 | tf_op jit(solution)/shard_map/pallas_call | solution.py:435
  2.3 3.3 %collective-permute-start = (f32[16,4,8,256]{3,2,1,0:T(8,128)S(1)}, f32[16,4,8,256]{3,2,1,0:T(8,128)S(1)}, u32[]{:S(2)}, u32[]{:S(2)}) collective-permute-start(f32[16,4,8,256]{3,2,1,0:T(8,128)S(1)} %get-tuple-element.36.own), channel_id=1, source_target_pairs={{0,1},{1,0},{2,3},{3,2},{4,5},{5,4},{6,7},{7,6},{8,9},{9,8},{10,11... | collective-permute-start | bytes 1572872 | tf_op jit(solution)/shard_map/ppermute | solution.py:421
  5.6 0.0 collective-permute-start.2
  5.6 1.5 %collective-permute-done.a1 = f32[16,4,8,256]{3,2,1,0:T(8,128)S(1)} collective-permute-done((f32[16,4,8,256]{3,2,1,0:T(8,128)S(1)}, f32[16,4,8,256]{3,2,1,0:T(8,128)S(1)}, u32[]{:S(2)}, u32[]{:S(2)}) %collective-permute-start) | collective-permute-done | bytes 524320 | tf_op jit(solution)/shard_map/ppermute | solution.py:421
  7.1 0.3 %shard_map.60 = (f32[2,13,3,4,8,256]{5,4,3,2,1,0:T(8,128)S(1)}, f32[16,2,4,8,256]{4,3,2,1,0:T(8,128)S(1)}, f32[4,3,4,8,256]{4,3,2,1,0:T(8,128)S(1)}, f32[13,4,8,256]{3,2,1,0:T(8,128)S(1)}) custom-call(s32[1]{0:T(128)} %bitcast.par, f32[6,8,256]{2,1,0:T(8,128)S(1)} %get-tuple-element.35.mod, ...), custom_call_target="tpu_custom_call", output_to_operand_aliasing={{0}: (4, {}), {1}: (5, {}), {2}: (6, {})} | custom-call | flops 1400000 | bytes 1000000 | tf_op jit(solution)/shard_map/pallas_call | solution.py:446
  7.4 0.3 %collective-permute-start.1 = (f32[13,4,8,256]{3,2,1,0:T(8,128)S(1)}, f32[13,4,8,256]{3,2,1,0:T(8,128)S(1)}, u32[]{:S(2)}, u32[]{:S(2)}) collective-permute-start(f32[13,4,8,256]{3,2,1,0:T(8,128)S(1)} %get-tuple-element.40), channel_id=1, source_target_pairs={{0,31},{1,2},{2,1},{3,4},{4,3},{5,6},{6,5},{7,8},{8,7},{9,10},{10,... | collective-permute-start | bytes 1277960 | tf_op jit(solution)/shard_map/ppermute | solution.py:421
  7.7 1.1 %shard_map.61 = (f32[2,13,3,4,8,256]{5,4,3,2,1,0:T(8,128)S(1)}, f32[16,2,4,8,256]{4,3,2,1,0:T(8,128)S(1)}, f32[4,3,4,8,256]{4,3,2,1,0:T(8,128)S(1)}, f32[13,4,8,...) custom-call(f32[2,13,3,4,8,256]{5,4,3,2,1,0:T(8,128)S(1)} %get-tuple-element, ...), custom_call_target="tpu_custom_call", output_to_operand_aliasing={{0}: (0, {}), {1}: (1, {}), {2}: (2, {})} | custom-call | flops 5600000 | bytes 4000000 | tf_op jit(solution)/shard_map/pallas_call | solution.py:450
  8.7 5.4 %collective-permute-done.2.b1 = f32[15,4,8,256]{3,2,1,0:T(8,128)S(1)} collective-permute-done((f32[15,4,8,256]{3,2,1,0:T(8,128)S(1)}, f32[15,4,8,256]{3,2,1,0:T(8,128)S(1)}, u32[]{:S(2)}, u32[]{:S(2)}) %collective-permute-start.2) | collective-permute-done | bytes 491552 | tf_op jit(solution)/shard_map/ppermute | solution.py:421
  14.1 1.7 %shard_map.62 = (f32[2,13,3,4,8,256]{5,4,3,2,1,0:T(8,128)S(1)}, f32[16,2,4,8,256]{4,3,2,1,0:T(8,128)S(1)}, f32[4,3,4,8,256]{4,3,2,1,0:T(8,128)S(1)}, f32[13,4,8,...) custom-call(s32[1]{0:T(128)} %bitcast.par, ...), custom_call_target="tpu_custom_call", output_to_operand_aliasing={{0}: (4, {}), {1}: (5, {}), {2}: (6, {}), {3}: (7, {})} | custom-call | flops 9800000 | bytes 7000000 | tf_op jit(solution)/shard_map/pallas_call | solution.py:453
  15.8 3.3 %collective-permute-start.3 = (f32[3,3,4,8,256]{4,3,2,1,0:T(8,128)S(1)}, f32[3,3,4,8,256]{4,3,2,1,0:T(8,128)S(1)}, u32[]{:S(2)}, u32[]{:S(2)}) collective-permute-start(f32[3,3,4,8,256]{4,3,2,1,0:T(8,128)S(1)} %get-tuple-element.50), channel_id=1, source_target_pairs={{0,1},{1,0},{2,3},{3,2},{4,5},{5,4},{6,7},{7,6},{8,9},{9,8},{10,11... | collective-permute-start | bytes 884744 | tf_op jit(solution)/shard_map/ppermute | solution.py:421
  19.1 1.0 %shard_map.63 = (f32[2,13,3,4,8,256]{5,4,3,2,1,0:T(8,128)S(1)}, f32[16,2,4,8,256]{4,3,2,1,0:T(8,128)S(1)}, f32[4,3,4,8,256]{4,3,2,1,0:T(8,128)S(1)}, f32[13,4,8,...) custom-call(f32[3,6,4,8,256]{4,3,2,1,0:T(8,128)S(1)} %get-tuple-elem, ...), custom_call_target="tpu_custom_call", output_to_operand_aliasing={{0}: (1, {}), {1}: (2, {}), {2}: (3, {}), {3}: (4, {})} | custom-call | flops 4200000 | bytes 3000000 | tf_op jit(solution)/shard_map/pallas_call | solution.py:462
  20.1 0.2 collective-permute-done.3.a3
  20.3 1.3 %shard_map.64 = (f32[2,13,3,4,8,256]{5,4,3,2,1,0:T(8,128)S(1)}, f32[16,2,4,8,256]{4,3,2,1,0:T(8,128)S(1)}, f32[4,3,4,8,256]{4,3,2,1,0:T(8,128)S(1)}, f32[13,4,8,...) custom-call(f32[3,3,4,8,256]{4,3,2,1,0:T(8,128)S(1)} %collective-per, ...), custom_call_target="tpu_custom_call", output_to_operand_aliasing={{0}: (1, {}), {1}: (2, {}), {2}: (3, {}), {3}: (4, {}), {4}... | custom-call | flops 6300000 | bytes 4500000 | tf_op jit(solution)/shard_map/pallas_call | solution.py:465
  21.6 0.0 collective-permute-done.1.b3
  21.6 3.3 %shard_map.65 = (f32[4,3,64,128]{3,2,1,0:T(8,128)}, f32[4,3,64,128]{3,2,1,0:T(8,128)}, f32[2,13,3,4,8,256]{5,4,3,2,1,0:T(8,128)S(1)}, f32[16,2,4,8,256]{4,3,2,1,...) custom-call(s32[1]{0:T(128)} %bitcast.par, ...), custom_call_target="tpu_custom_call", output_to_operand_aliasing={{2}: (4, {}), {3}: (5, {}), {4}: (6, {}), {5}: (7, {})} | custom-call | flops 16800000 | bytes 12000000 | tf_op jit(solution)/shard_map/pallas_call | solution.py:468
Async XLA Ops:
  2.3 4.8 %collective-permute-start = (f32[16,4,8,256]{3,2,1,0:T(8,128)S(1)}, f32[16,4,8,256]{3,2,1,0:T(8,128)S(1)}, u32[]{:S(2)}, u32[]{:S(2)}) collective-permute-start(f32[16,4,8,256]{3,2,1,0:T(8,128)S(1)} %get-tuple-element.36.own), channel_id=1, source_target_pairs={{0,1},{1,0},{2,3},{3,2},{4,5},{5,4},{6,7},{7,6},{8,9},{9,8},{10,11... | collective-permute-start | bytes 1572872 | tf_op jit(solution)/shard_map/ppermute | solution.py:421
  5.6 8.6 %collective-permute-start.2 = (f32[15,4,8,256]{3,2,1,0:T(8,128)S(1)}, f32[15,4,8,256]{3,2,1,0:T(8,128)S(1)}, u32[]{:S(2)}, u32[]{:S(2)}) collective-permute-start(f32[15,4,8,256]{3,2,1,0:T(8,128)S(1)} %get-tuple-element.41), channel_id=1, source_target_pairs={{0,31},{1,2},{2,1},{3,4},{4,3},{5,6},{6,5},{7,8},{8,7},{9,10},{10,... | collective-permute-start | bytes 1474568 | tf_op jit(solution)/shard_map/ppermute | solution.py:421
  7.4 14.2 %collective-permute-start.1 = (f32[13,4,8,256]{3,2,1,0:T(8,128)S(1)}, f32[13,4,8,256]{3,2,1,0:T(8,128)S(1)}, u32[]{:S(2)}, u32[]{:S(2)}) collective-permute-start(f32[13,4,8,256]{3,2,1,0:T(8,128)S(1)} %get-tuple-element.40), channel_id=1, source_target_pairs={{0,31},{1,2},{2,1},{3,4},{4,3},{5,6},{6,5},{7,8},{8,7},{9,10},{10,... | collective-permute-start | bytes 1277960 | tf_op jit(solution)/shard_map/ppermute | solution.py:421
  15.8 4.5 %collective-permute-start.3 = (f32[3,3,4,8,256]{4,3,2,1,0:T(8,128)S(1)}, f32[3,3,4,8,256]{4,3,2,1,0:T(8,128)S(1)}, u32[]{:S(2)}, u32[]{:S(2)}) collective-permute-start(f32[3,3,4,8,256]{4,3,2,1,0:T(8,128)S(1)} %get-tuple-element.50), channel_id=1, source_target_pairs={{0,1},{1,0},{2,3},{3,2},{4,5},{5,4},{6,7},{7,6},{8,9},{9,8},{10,11... | collective-permute-start | bytes 884744 | tf_op jit(solution)/shard_map/ppermute | solution.py:421

commit v5 on v4

--- a/solution.py
+++ b/solution.py
@@ -110,10 +110,11 @@
     stress(prev, tuple(pltpu.roll(v, 7, 0) for v in first[:6]), 3)
 
 
-def node_sums(st, m, r, above, below, top):
+def node_sums(st, m, r, above, below, top, base):
     upper = st.at[m + L0] if top is None else top
     new = [upper[i, r] if above else None for i in range(6)]
-    old = [st[m - 1 + L0, i, r] if below else None for i in range(6)]
+    lower = st.at[m - 1 + L0] if base is None else base
+    old = [lower[i, r] if below else None for i in range(6)]
 
     def plus(i):
         return new[i] if not below else old[i] if not above else new[i] + old[i]
@@ -130,7 +131,7 @@
     )
 
 
-def node_step(st, m, finish, above=True, below=True, top=None):
+def node_step(st, m, finish, above=True, below=True, top=None, base=None):
     first = prev = None
 
     def out(pq, pp, ph, r):
@@ -140,7 +141,7 @@
             finish(m, c, r, (g - hh) + y_prev(g + hh))
 
     for r in range(4):
-        pq = node_sums(st, m, r, above, below, top)
+        pq = node_sums(st, m, r, above, below, top, base)
         if r == 0:
             first = pq
         else:
@@ -150,7 +151,7 @@
     out(first, tuple(map(roll, prev[0])), tuple(map(roll, prev[2])), 0)
 
 
-def advance(refs, s, lo, hi, save=None, top=None, after=None):
+def advance(refs, s, lo, hi, save=None, top=None, after=None, base=None, keep=None):
     R, W, LM, U, sm, st = refs
     src, dst = s % 2, (s + 1) % 2
 
@@ -168,14 +169,17 @@
 
     def layer(m):
         if m < hi or (m == hi and top is None):
-            stress_step(sm, st, LM, m, get)
-
-    y_stage(sm, get, lo - 1)
-    stress_step(sm, st, LM, lo - 1, get, save)
+            stress_step(sm, st, LM, m, get, keep if m == hi else None)
+
+    if base is None:
+        y_stage(sm, get, lo - 1)
+        stress_step(sm, st, LM, lo - 1, get, save)
+    else:
+        y_stage(sm, get, lo)
     layer(lo)
     for m in range(lo, hi + 1):
         layer(m + 1)
-        node_step(st, m, finisher(0 <= m < OWN), top=top if m == hi else None)
+        node_step(st, m, finisher(0 <= m < OWN), top=top if m == hi else None, base=base if m == lo else None)
         if after is not None:
             after(m)
 
@@ -340,7 +344,7 @@
     advance(refs, 0, -2, -2, ES.at[0], e1.at[0])
     advance(refs, 1, -1, -1, ES.at[1], e1.at[1])
     advance(refs, 2, 0, 0, ES.at[2], e1.at[2])
-    advance(refs, 3, 1, 2, ES.at[3])
+    advance(refs, 3, 1, 2, ES.at[3], keep=ES.at[5])
 
 
 def kernel_inner(a3, r_in, lm_in, u_in, w_in, e_in, R, LM, U, W, ES, sm, st):
@@ -348,7 +352,7 @@
         for c in range(3):
             R[1, 4 + j + N0, c] = flipped(a3[2 - j, c], c)
     refs = (R, W, LM, U, sm, st)
-    advance(refs, 3, 3, 5)
+    advance(refs, 3, 3, 5, base=ES.at[5])
     advance(refs, 4, 2, 4, ES.at[4])
     advance(refs, 5, 3, 3, ES.at[5])
 

time: 25 us -> 24.9 us (level)
  no operation moved by 1% of the time
where the time goes in v5:
time: 24.9 us; the launch traced here: 24.8 us
  Pallas kernels  10.1 us (41%)
  waiting for transfers between devices  7.09 us (28%)
  starting transfers between devices  6.91 us (28%)
  between operations  0.68 us (3%)
    ppermute x4, waiting for transfers between devices, send(): return lax.ppermute(v, 'slab', pairs)  7.09 us
    ppermute x4, starting transfers between devices, send(): return lax.ppermute(v, 'slab', pairs)  6.91 us
    pallas_call x1, Pallas kernels, sweeps(): call(kernel_last, [SMEM] + [VMEM] * 7, (whole, whole) + state, [sm, st],...  3.29 us
    pallas_call x1, Pallas kernels, sweeps(): call(kernel_mid, [SMEM] + [VMEM] * 7, state + (f32(3, 6), f32(3, 3)), [(3...  1.66 us
    pallas_call x1, Pallas kernels, sweeps(): call(kernel_own, [SMEM] + [HBM] * 4, (R, LM, U, f32(16), f32(15), six), [...  1.63 us
    pallas_call x1, Pallas kernels, sweeps(): call(kernel_inner, [VMEM] * 6, state + (f32(6, 6),), [sm, st], {1: 0, 2:...  1.23 us
    pallas_call x1, Pallas kernels, sweeps(): call(kernel_near, [VMEM] * 3, state + (f32(2, 6),), [sm, st], {0: 0, 1: 1...  1.07 us
    pallas_call x1, Pallas kernels, sweeps(): call(kernel_lead, [VMEM] * 5, state + (f32(6, 6),), [sm, st], {1: 0, 2: 1...  1.02 us
  transfers between devices with their start and end apart: 4, of which 3 were waited for; matrix products, arithmetic and copies ran while one was open for 0% of the time, Pallas kernels for 21%

profile of v5, /device:TPU:1, one launch (start us, length us, event | category | flops | bytes accessed | tf_op | source)
XLA Modules:
  0.0 24.8 jit_solution(43136761269079206)
XLA Ops:
  0.6 1.6 %shard_map.59 = (f32[2,13,3,4,8,256]{5,4,3,2,1,0:T(8,128)S(1)}, f32[16,2,4,8,256]{4,3,2,1,0:T(8,128)S(1)}, f32[4,3,4,8,256]{4,3,2,1,0:T(8,128)S(1)}, f32[16,4,8,...) custom-call(s32[1]{0:T(128)} %bitcast.par, f32[2,3]{1,0:T(2,128)} %mod_h.1, ...), custom_call_target="tpu_custom_call" | custom-call | flops 2800000 | bytes 2000000 | tf_op jit(solution)/shard_map/pallas_call | solution.py:439
  2.3 3.3 %collective-permute-start = (f32[16,4,8,256]{3,2,1,0:T(8,128)S(1)}, f32[16,4,8,256]{3,2,1,0:T(8,128)S(1)}, u32[]{:S(2)}, u32[]{:S(2)}) collective-permute-start(f32[16,4,8,256]{3,2,1,0:T(8,128)S(1)} %get-tuple-element.36.own), channel_id=1, source_target_pairs={{0,1},{1,0},{2,3},{3,2},{4,5},{5,4},{6,7},{7,6},{8,9},{9,8},{10,11... | collective-permute-start | bytes 1572872 | tf_op jit(solution)/shard_map/ppermute | solution.py:425
  5.6 0.0 collective-permute-start.2
  5.6 1.5 %collective-permute-done.a1 = f32[16,4,8,256]{3,2,1,0:T(8,128)S(1)} collective-permute-done((f32[16,4,8,256]{3,2,1,0:T(8,128)S(1)}, f32[16,4,8,256]{3,2,1,0:T(8,128)S(1)}, u32[]{:S(2)}, u32[]{:S(2)}) %collective-permute-start) | collective-permute-done | bytes 524320 | tf_op jit(solution)/shard_map/ppermute | solution.py:425
  7.1 0.3 %shard_map.60 = (f32[2,13,3,4,8,256]{5,4,3,2,1,0:T(8,128)S(1)}, f32[16,2,4,8,256]{4,3,2,1,0:T(8,128)S(1)}, f32[4,3,4,8,256]{4,3,2,1,0:T(8,128)S(1)}, f32[13,4,8,256]{3,2,1,0:T(8,128)S(1)}) custom-call(s32[1]{0:T(128)} %bitcast.par, f32[6,8,256]{2,1,0:T(8,128)S(1)} %get-tuple-element.35.mod, ...), custom_call_target="tpu_custom_call", output_to_operand_aliasing={{0}: (4, {}), {1}: (5, {}), {2}: (6, {})} | custom-call | flops 1400000 | bytes 1000000 | tf_op jit(solution)/shard_map/pallas_call | solution.py:450
  7.4 0.3 %collective-permute-start.1 = (f32[13,4,8,256]{3,2,1,0:T(8,128)S(1)}, f32[13,4,8,256]{3,2,1,0:T(8,128)S(1)}, u32[]{:S(2)}, u32[]{:S(2)}) collective-permute-start(f32[13,4,8,256]{3,2,1,0:T(8,128)S(1)} %get-tuple-element.40), channel_id=1, source_target_pairs={{0,31},{1,2},{2,1},{3,4},{4,3},{5,6},{6,5},{7,8},{8,7},{9,10},{10,... | collective-permute-start | bytes 1277960 | tf_op jit(solution)/shard_map/ppermute | solution.py:425
  7.7 1.1 %shard_map.61 = (f32[2,13,3,4,8,256]{5,4,3,2,1,0:T(8,128)S(1)}, f32[16,2,4,8,256]{4,3,2,1,0:T(8,128)S(1)}, f32[4,3,4,8,256]{4,3,2,1,0:T(8,128)S(1)}, f32[13,4,8,...) custom-call(f32[2,13,3,4,8,256]{5,4,3,2,1,0:T(8,128)S(1)} %get-tuple-element, ...), custom_call_target="tpu_custom_call", output_to_operand_aliasing={{0}: (0, {}), {1}: (1, {}), {2}: (2, {})} | custom-call | flops 5600000 | bytes 4000000 | tf_op jit(solution)/shard_map/pallas_call | solution.py:454
  8.7 5.4 %collective-permute-done.2.b1 = f32[15,4,8,256]{3,2,1,0:T(8,128)S(1)} collective-permute-done((f32[15,4,8,256]{3,2,1,0:T(8,128)S(1)}, f32[15,4,8,256]{3,2,1,0:T(8,128)S(1)}, u32[]{:S(2)}, u32[]{:S(2)}) %collective-permute-start.2) | collective-permute-done | bytes 491552 | tf_op jit(solution)/shard_map/ppermute | solution.py:425
  14.1 1.7 %shard_map.62 = (f32[2,13,3,4,8,256]{5,4,3,2,1,0:T(8,128)S(1)}, f32[16,2,4,8,256]{4,3,2,1,0:T(8,128)S(1)}, f32[4,3,4,8,256]{4,3,2,1,0:T(8,128)S(1)}, f32[13,4,8,...) custom-call(s32[1]{0:T(128)} %bitcast.par, ...), custom_call_target="tpu_custom_call", output_to_operand_aliasing={{0}: (4, {}), {1}: (5, {}), {2}: (6, {}), {3}: (7, {})} | custom-call | flops 9800000 | bytes 7000000 | tf_op jit(solution)/shard_map/pallas_call | solution.py:457
  15.8 3.3 %collective-permute-start.3 = (f32[3,3,4,8,256]{4,3,2,1,0:T(8,128)S(1)}, f32[3,3,4,8,256]{4,3,2,1,0:T(8,128)S(1)}, u32[]{:S(2)}, u32[]{:S(2)}) collective-permute-start(f32[3,3,4,8,256]{4,3,2,1,0:T(8,128)S(1)} %get-tuple-element.50), channel_id=1, source_target_pairs={{0,1},{1,0},{2,3},{3,2},{4,5},{5,4},{6,7},{7,6},{8,9},{9,8},{10,11... | collective-permute-start | bytes 884744 | tf_op jit(solution)/shard_map/ppermute | solution.py:425
  19.1 1.0 %shard_map.63 = (f32[2,13,3,4,8,256]{5,4,3,2,1,0:T(8,128)S(1)}, f32[16,2,4,8,256]{4,3,2,1,0:T(8,128)S(1)}, f32[4,3,4,8,256]{4,3,2,1,0:T(8,128)S(1)}, f32[13,4,8,...) custom-call(f32[3,6,4,8,256]{4,3,2,1,0:T(8,128)S(1)} %get-tuple-elem, ...), custom_call_target="tpu_custom_call", output_to_operand_aliasing={{0}: (1, {}), {1}: (2, {}), {2}: (3, {}), {3}: (4, {})} | custom-call | flops 4200000 | bytes 3000000 | tf_op jit(solution)/shard_map/pallas_call | solution.py:466
  20.1 0.2 collective-permute-done.3.a3
  20.3 1.2 %shard_map.64 = (f32[2,13,3,4,8,256]{5,4,3,2,1,0:T(8,128)S(1)}, f32[16,2,4,8,256]{4,3,2,1,0:T(8,128)S(1)}, f32[4,3,4,8,256]{4,3,2,1,0:T(8,128)S(1)}, f32[13,4,8,...) custom-call(f32[3,3,4,8,256]{4,3,2,1,0:T(8,128)S(1)} %collective-per, ...), custom_call_target="tpu_custom_call", output_to_operand_aliasing={{0}: (1, {}), {1}: (2, {}), {2}: (3, {}), {3}: (4, {}), {4}... | custom-call | flops 6300000 | bytes 4500000 | tf_op jit(solution)/shard_map/pallas_call | solution.py:469
  21.5 0.0 collective-permute-done.1.b3
  21.6 3.3 %shard_map.65 = (f32[4,3,64,128]{3,2,1,0:T(8,128)}, f32[4,3,64,128]{3,2,1,0:T(8,128)}, f32[2,13,3,4,8,256]{5,4,3,2,1,0:T(8,128)S(1)}, f32[16,2,4,8,256]{4,3,2,1,...) custom-call(s32[1]{0:T(128)} %bitcast.par, ...), custom_call_target="tpu_custom_call", output_to_operand_aliasing={{2}: (4, {}), {3}: (5, {}), {4}: (6, {}), {5}: (7, {})} | custom-call | flops 16800000 | bytes 12000000 | tf_op jit(solution)/shard_map/pallas_call | solution.py:472
Async XLA Ops:
  2.3 4.8 %collective-permute-start = (f32[16,4,8,256]{3,2,1,0:T(8,128)S(1)}, f32[16,4,8,256]{3,2,1,0:T(8,128)S(1)}, u32[]{:S(2)}, u32[]{:S(2)}) collective-permute-start(f32[16,4,8,256]{3,2,1,0:T(8,128)S(1)} %get-tuple-element.36.own), channel_id=1, source_target_pairs={{0,1},{1,0},{2,3},{3,2},{4,5},{5,4},{6,7},{7,6},{8,9},{9,8},{10,11... | collective-permute-start | bytes 1572872 | tf_op jit(solution)/shard_map/ppermute | solution.py:425
  5.6 8.6 %collective-permute-start.2 = (f32[15,4,8,256]{3,2,1,0:T(8,128)S(1)}, f32[15,4,8,256]{3,2,1,0:T(8,128)S(1)}, u32[]{:S(2)}, u32[]{:S(2)}) collective-permute-start(f32[15,4,8,256]{3,2,1,0:T(8,128)S(1)} %get-tuple-element.41), channel_id=1, source_target_pairs={{0,31},{1,2},{2,1},{3,4},{4,3},{5,6},{6,5},{7,8},{8,7},{9,10},{10,... | collective-permute-start | bytes 1474568 | tf_op jit(solution)/shard_map/ppermute | solution.py:425
  7.4 14.2 %collective-permute-start.1 = (f32[13,4,8,256]{3,2,1,0:T(8,128)S(1)}, f32[13,4,8,256]{3,2,1,0:T(8,128)S(1)}, u32[]{:S(2)}, u32[]{:S(2)}) collective-permute-start(f32[13,4,8,256]{3,2,1,0:T(8,128)S(1)} %get-tuple-element.40), channel_id=1, source_target_pairs={{0,31},{1,2},{2,1},{3,4},{4,3},{5,6},{6,5},{7,8},{8,7},{9,10},{10,... | collective-permute-start | bytes 1277960 | tf_op jit(solution)/shard_map/ppermute | solution.py:425
  15.8 4.5 %collective-permute-start.3 = (f32[3,3,4,8,256]{4,3,2,1,0:T(8,128)S(1)}, f32[3,3,4,8,256]{4,3,2,1,0:T(8,128)S(1)}, u32[]{:S(2)}, u32[]{:S(2)}) collective-permute-start(f32[3,3,4,8,256]{4,3,2,1,0:T(8,128)S(1)} %get-tuple-element.50), channel_id=1, source_target_pairs={{0,1},{1,0},{2,3},{3,2},{4,5},{5,4},{6,7},{7,6},{8,9},{9,8},{10,11... | collective-permute-start | bytes 884744 | tf_op jit(solution)/shard_map/ppermute | solution.py:425
